TPU v7x, 32 devices: a whole 2x2x4 slice. The times are simulated.
32 devices in a mesh: ctx: 16 (over z, y, x), head: 2 (over core).
Axes of the slice: x: 2, y: 2, z: 4, core: 2. Of those that a mesh axis runs over, the one named last changes fastest.
Arguments:
- banded_queries: bfloat16 [4096, 4096], P('ctx', 'head'), may hold values from -11.5 to 11.5
- banded_keys: bfloat16 [4096, 512], P('ctx', 'head'), may hold values from -11.5 to 11.5
- banded_values: bfloat16 [4096, 512], P('ctx', 'head'), may hold values from -6 to 6
- full_queries: bfloat16 [4096, 4096], P('ctx', 'head'), may hold values from -11.5 to 11.5
- full_keys: bfloat16 [4096, 512], P('ctx', 'head'), may hold values from -11.5 to 11.5
- full_values: bfloat16 [4096, 512], P('ctx', 'head'), may hold values from -6 to 6
- segment_ids: int32 [4096], P('ctx'), may hold values from 0 to 4095, as said below
- position_ids: int32 [4096], P('ctx'), may hold values from 0 to 8189, as said below
- out_weight: bfloat16 [4096, 2880], P('head'), may hold values from -0.09375 to 0.09375
Outputs:
- banded_out: bfloat16 [4096, 4096], P('ctx', 'head')
- projected: bfloat16 [4096, 2880], P(('ctx', 'head'))
Inputs may be any that keep to these rules, and one draw needn't show every extreme that they name: `segment_ids`: never falling; a document's id is the index of its last token; every document holds 1 to 3072 tokens, and one holds exactly 3072. `position_ids`: within a document they rise by 1 or 2 from one token to the next.
All inputs are finite; a program needn't handle non-finite values.
Results may differ from a plain program's by a relative error of at most 0.015.
The roundings to bfloat16 on the way count: a program that leaves them out, or rounds other values in their place, can miss the bound.
Values may be sent and summed in bfloat16 or wider, within the bound.
No kernel may reach another device: no remote copies, remote signals or barrier semaphores. Data moves between devices by JAX's collectives and lax.ppermute only.
A program may use at most 64 MiB of HBM per device.

v0:
```python
import functools

import jax
import jax.numpy as jnp
from jax import lax
from jax.experimental import pallas as pl
from jax.experimental.pallas import tpu as pltpu
from jax.sharding import PartitionSpec as P


HEAD_DIM = 64
WINDOW = 128
REACH = 12
PLANE = 4
PAD = 16
AUG = 2 * HEAD_DIM
META = 16
BACK = 2
PICK_X = BACK + REACH // PLANE + 1
PICK_Y = PICK_X + 1
SIDE0 = PICK_X + 2
LATER = PICK_X + 3

theta_base = 150000.0
neg_fill = -1e30
to_log2 = HEAD_DIM ** (-0.5) * 1.4426950408889634

f32 = jnp.float32
bf16 = jnp.bfloat16
VM = pl.BlockSpec(memory_space=pltpu.VMEM)
SM = pl.BlockSpec(memory_space=pltpu.SMEM)


def al(start, size):
    return pl.ds(pl.multiple_of(start, size), size)


def rotate_rows(rows, cosine, sine_term):
    half = HEAD_DIM // 2
    out = []
    for at in range(0, rows.shape[0], HEAD_DIM):
        leading = rows[at : at + half]
        trailing = rows[at + half : at + HEAD_DIM]
        out.append(leading * cosine - trailing * sine_term)
        out.append(trailing * cosine + leading * sine_term)
    return jnp.concatenate(out, axis=0).astype(bf16)


def write_block(block, rows, id_rows, cos, sin):
    width = rows.shape[0] // 2
    block[0:width, :] = rotate_rows(rows[:width], cos, sin)
    block[width : width + PAD, :] = id_rows
    block[width + PAD :, :] = rows[width:].astype(bf16)


def prepare_kernel(base, side, frequency, kv, ids_pos, block, band_block, rim, meta, cosine, sine):
    tokens = kv.shape[0]
    angles = ids_pos[1:2, :].astype(f32) * frequency[...]
    cos, sin = jnp.cos(angles), jnp.sin(angles)
    cosine[...] = cos
    sine[...] = sin
    ids = ids_pos[0:1, :]
    shifted = ids + 1
    row = lax.broadcasted_iota(jnp.int32, (PAD, tokens), 0)
    high = jnp.broadcast_to(shifted >> 7, (PAD, tokens))
    low = jnp.broadcast_to(shifted & 127, (PAD, tokens))
    id_rows = jnp.where(row == 0, high, jnp.where(row == 1, low, 0)).astype(f32).astype(bf16)
    half = kv.shape[1] // 2
    write_block(block, kv[:, :half].astype(f32).T, id_rows, cos, sin)
    write_block(band_block, kv[:, half:].astype(f32).T, id_rows, cos, sin)
    rim[...] = band_block[:, tokens - WINDOW :]
    ids_f = ids.astype(f32)
    across = jnp.broadcast_to(ids_f, (tokens, tokens))
    down = across.T
    before = jnp.max(jnp.where(down < across, down, -1.0), axis=0, keepdims=True)
    first = before < 0.0
    begin = jnp.where(first, 0.0, before + 1.0 - base[0].astype(f32))
    here = base[0] // tokens
    plane = here // PLANE
    farthest = REACH // PLANE
    rows = [begin, first.astype(f32), ids_f + 1.0]
    rows += [plane >= back for back in range(1, farthest + 1)]
    rows += [(here % 2 == 1) | (plane >= farthest), (here // 2 % 2 == 1) | (plane >= farthest)]
    rows += [side[0] == 0, here > 0]
    mrow = lax.broadcasted_iota(jnp.int32, meta.shape, 0)
    total = jnp.zeros(meta.shape, f32)
    for i, value in enumerate(rows):
        value = jnp.where(value, 1.0, 0.0) if value.dtype == jnp.bool_ else value
        total = jnp.where(mrow == i, jnp.broadcast_to(value, meta.shape), total)
    meta[...] = total


def prepare(base, side, frequency, kv, ids_pos):
    tokens, every = kv.shape
    height = every // 2 + PAD
    half = HEAD_DIM // 2
    return pl.pallas_call(
        prepare_kernel,
        out_shape=(
            jax.ShapeDtypeStruct((height, tokens), bf16),
            jax.ShapeDtypeStruct((height, tokens), bf16),
            jax.ShapeDtypeStruct((height, WINDOW), bf16),
            jax.ShapeDtypeStruct((META, tokens), f32),
            jax.ShapeDtypeStruct((half, tokens), f32),
            jax.ShapeDtypeStruct((half, tokens), f32),
        ),
        in_specs=[SM] * 2 + [VM] * 3,
        out_specs=(VM,) * 6,
        compiler_params=pltpu.CompilerParams(vmem_limit_bytes=8 << 20),
        name="prepare",
    )(base, side, frequency, kv, ids_pos)


def two_deep(units, step, s0, s1, x0, x1):
    even, odd = (s0, x0), (s1, x1)
    step(-1, None, even)

    def pair(i, _):
        step(2 * i, even, odd)
        step(2 * i + 1, odd, even)
        return 0

    lax.fori_loop(0, units // 2 - 1, pair, 0)
    step(units - 2, even, odd)
    step(units - 1, odd, None)


def by_tiles(tiles, scores, outs):
    def step(u, now, then):
        for tile in range(tiles):
            if then is not None:
                scores(u + 1, tile, *then)
            if now is not None:
                outs(u, tile, *now)

    return step


def column_peak(s):
    return jnp.broadcast_to(jnp.max(s, axis=0, keepdims=True), (8, s.shape[1]))


def transposed_keys(rows, extra):
    return jnp.concatenate([rows.astype(f32), extra], axis=0).T.astype(bf16)


def ids_of(rows):
    rows = rows.astype(f32)
    return rows[0:1] * 128.0 + rows[1:2]


def mask_rows(ids, own_id, present):
    bar = jnp.where((ids < own_id) | jnp.logical_not(present), neg_fill, 0.0)
    row = lax.broadcasted_iota(jnp.int32, (HEAD_DIM, ids.shape[1]), 0)
    return jnp.where(row == 0, jnp.broadcast_to(bar, row.shape), jnp.where(row == 1, 1.0, 0.0))


def rotate_into(src, dst, cos, sin):
    wide = src.shape[1]
    step = min(wide, 4 * AUG)
    for at in range(0, wide, step):
        dst[at : at + step, :] = rotate_rows(src[:, at : at + step].astype(f32).T, cos, sin)


def own_kernel(group, fq, bq, cosine, sine, block, meta, fqt, bqt, peak, total, accum, keys, bias, s0, s1, x0, x1):
    tokens, wide = fq.shape
    width = wide // group
    kv = width // HEAD_DIM
    rotate_into(fq, fqt, cosine[...], sine[...])
    zero = jnp.zeros((HEAD_DIM, tokens), f32)
    for h in range(kv):
        keys[h * tokens : (h + 1) * tokens, :] = transposed_keys(block[h * HEAD_DIM : (h + 1) * HEAD_DIM, :], zero)
    begin = jnp.broadcast_to(meta[0:1, :], (tokens, tokens)).astype(jnp.int32)
    r = lax.broadcasted_iota(jnp.int32, (tokens, tokens), 0)
    t = lax.broadcasted_iota(jnp.int32, (tokens, tokens), 1)
    bias[...] = jnp.where((r >= begin) & (r <= t), 0.0, neg_fill)
    several = s0.shape[0] // tokens

    def scores(u, g, buf, x):
        h = u * several // group
        k = keys[al(h * tokens, tokens), :][:, :HEAD_DIM]
        q = fqt[al((u * several + g) * HEAD_DIM, HEAD_DIM), :]
        s = jnp.dot(k, q, preferred_element_type=f32) + bias[...]
        buf[g * tokens : (g + 1) * tokens, :] = s
        x[8 * g : 8 * g + 8, :] = column_peak(s)

    def outs(u, g, buf, x):
        h = u * several // group
        v = block[pl.ds(pl.multiple_of(width + PAD + h * HEAD_DIM, PAD), HEAD_DIM), :]
        at = u * several + g
        m = x[8 * g : 8 * g + 1, :]
        p = jnp.exp2(buf[g * tokens : (g + 1) * tokens, :] * to_log2 - m * to_log2)
        peak[pl.ds(at, 1), :] = m
        total[pl.ds(at, 1), :] = jnp.sum(p, axis=0, keepdims=True)
        accum[al(at * HEAD_DIM, HEAD_DIM), :] = jnp.dot(v, p.astype(bf16), preferred_element_type=f32)

    two_deep(wide // HEAD_DIM // several, by_tiles(several, scores, outs), s0, s1, x0, x1)
    rotate_into(bq, bqt, cosine[...], sine[...])


def own(group, fq, bq, cosine, sine, block, meta):
    tokens, wide = fq.shape
    heads = wide // HEAD_DIM
    kv = heads // group
    several = 4
    return pl.pallas_call(
        functools.partial(own_kernel, group),
        out_shape=(
            jax.ShapeDtypeStruct((wide, tokens), bf16),
            jax.ShapeDtypeStruct((wide, tokens), bf16),
            jax.ShapeDtypeStruct((heads, tokens), f32),
            jax.ShapeDtypeStruct((heads, tokens), f32),
            jax.ShapeDtypeStruct((wide, tokens), f32),
        ),
        in_specs=[VM] * 6,
        out_specs=(VM,) * 5,
        scratch_shapes=[
            pltpu.VMEM((kv * tokens, AUG), bf16),
            pltpu.VMEM((tokens, tokens), f32),
            pltpu.VMEM((several * tokens, tokens), f32),
            pltpu.VMEM((several * tokens, tokens), f32),
            pltpu.VMEM((8 * several, tokens), f32),
            pltpu.VMEM((8 * several, tokens), f32),
        ],
        compiler_params=pltpu.CompilerParams(vmem_limit_bytes=16 << 20),
        cost_estimate=pl.CostEstimate(
            flops=4 * heads * tokens * tokens * HEAD_DIM * 4, transcendentals=heads * tokens * tokens, bytes_accessed=12 * wide * tokens
        ),
        name="own",
    )(fq, bq, cosine, sine, block, meta)


def band_kernel(group, bqt, block, rim, meta, out, keys, vals, bias, s0, s1, x0, x1):
    wide, tokens = bqt.shape
    width = wide // group
    kv = width // HEAD_DIM
    span = tokens + WINDOW
    tile = 2 * WINDOW
    zero = jnp.zeros((HEAD_DIM, tokens), f32)
    for h in range(kv):
        rows = slice(h * HEAD_DIM, (h + 1) * HEAD_DIM)
        keys[h * span : h * span + WINDOW, :] = transposed_keys(rim[rows, :], zero[:, :WINDOW])
        keys[h * span + WINDOW : (h + 1) * span, :] = transposed_keys(block[rows, :], zero)
    vals[:, :WINDOW] = rim[width + PAD :, :]
    vals[:, WINDOW:] = block[width + PAD :, :]
    own_id = jnp.min(meta[2:3, :])
    barred = (ids_of(rim[width : width + PAD, :]) < own_id) | (meta[LATER : LATER + 1, :WINDOW] == 0.0)
    barred = jnp.sum(barred.astype(f32))
    begin = meta[0:1, :]
    first = meta[1:2, :]
    r = lax.broadcasted_iota(jnp.int32, (tile, tile), 0).astype(f32)
    t = (lax.broadcasted_iota(jnp.int32, (1, tile), 1) & (WINDOW - 1)).astype(f32)
    halves = tokens // WINDOW
    for half in range(halves):
        lo = begin + float(WINDOW - half * WINDOW)
        if half == 0:
            lo = jnp.where(first > 0.0, barred, lo)
        lo = lo[:, half * WINDOW : (half + 1) * WINDOW]
        low = jnp.maximum(jnp.concatenate([lo, lo], axis=1), t + 1.0)
        bias[half * tile : (half + 1) * tile, :] = jnp.where((r >= low) & (r <= t + WINDOW), 0.0, neg_fill)
    pairs = group // 2
    several = s0.shape[0] // tile // halves

    def scores(u, at, buf, x):
        half, g = divmod(at, several)
        h = u * several // pairs
        k = keys[pl.ds(pl.multiple_of(h * span + half * WINDOW, WINDOW), tile), :][:, :HEAD_DIM]
        q = bqt[al((u * several + g) * AUG, AUG), :][:, half * WINDOW : (half + 1) * WINDOW]
        q = jnp.concatenate([q[:HEAD_DIM], q[HEAD_DIM:]], axis=1)
        s = jnp.dot(k, q, preferred_element_type=f32) + bias[half * tile : (half + 1) * tile, :]
        buf[at * tile : (at + 1) * tile, :] = s
        x[8 * at : 8 * at + 8, :] = column_peak(s)

    def outs(u, at, buf, x):
        half, g = divmod(at, several)
        h = u * several // pairs
        v = vals[al(h * HEAD_DIM, HEAD_DIM), half * WINDOW : half * WINDOW + tile]
        m = x[8 * at : 8 * at + 1, :]
        p = jnp.exp2(buf[at * tile : (at + 1) * tile, :] * to_log2 - m * to_log2)
        total = jnp.sum(p, axis=0, keepdims=True)
        o = jnp.dot(v, p.astype(bf16), preferred_element_type=f32) / total
        o = jnp.concatenate([o[:, :WINDOW], o[:, WINDOW:]], axis=0)
        out[half * WINDOW : (half + 1) * WINDOW, al((u * several + g) * AUG, AUG)] = o.T.astype(bf16)

    two_deep(kv * pairs // several, by_tiles(halves * several, scores, outs), s0, s1, x0, x1)


def band(group, bqt, block, rim, meta):
    wide, tokens = bqt.shape
    kv = wide // group // HEAD_DIM
    span = tokens + WINDOW
    several = 2
    tiles = several * (tokens // WINDOW)
    return pl.pallas_call(
        functools.partial(band_kernel, group),
        out_shape=jax.ShapeDtypeStruct((tokens, wide), bf16),
        in_specs=[VM] * 4,
        out_specs=VM,
        scratch_shapes=[
            pltpu.VMEM((kv * span, AUG), bf16),
            pltpu.VMEM((kv * HEAD_DIM, span), bf16),
            pltpu.VMEM((tokens // WINDOW * 2 * WINDOW, 2 * WINDOW), f32),
            pltpu.VMEM((tiles * 2 * WINDOW, 2 * WINDOW), f32),
            pltpu.VMEM((tiles * 2 * WINDOW, 2 * WINDOW), f32),
            pltpu.VMEM((8 * tiles, 2 * WINDOW), f32),
            pltpu.VMEM((8 * tiles, 2 * WINDOW), f32),
        ],
        compiler_params=pltpu.CompilerParams(vmem_limit_bytes=16 << 20),
        cost_estimate=pl.CostEstimate(
            flops=4 * wide * tokens * 2 * WINDOW * 4, transcendentals=wide // HEAD_DIM * tokens * 2 * WINDOW, bytes_accessed=4 * wide * tokens
        ),
        name="band",
    )(bqt, block, rim, meta)


def remote_update(group, fqt, shards, meta, state_in, state_out, keys, s0, s1, x0, x1):
    wide, tokens = fqt.shape
    width = wide // group
    kv = width // HEAD_DIM
    span = len(shards) * tokens
    peak_in, total_in, accum_in = state_in
    peak, total, accum = state_out
    own_id = jnp.min(meta[2:3, :])
    for b, (kref, krow, _, _, flag) in enumerate(shards):
        extra = mask_rows(ids_of(kref[krow + width : krow + width + PAD, :]), own_id, meta[flag : flag + 1, :] > 0.0)
        for h in range(kv):
            rows = kref[krow + h * HEAD_DIM : krow + (h + 1) * HEAD_DIM, :]
            keys[h * span + b * tokens : h * span + (b + 1) * tokens, :] = transposed_keys(rows, extra)
    row = lax.broadcasted_iota(jnp.int32, (HEAD_DIM, tokens), 0)
    other = jnp.where(meta[1:2, :] > 0.0, 0.0, neg_fill)
    query_rows = jnp.where(row == 0, 1.0, jnp.where(row == 1, jnp.broadcast_to(other, row.shape), 0.0)).astype(bf16)

    several = s0.shape[0] // span

    def step(u, now, then):
        h = u * several // group
        h_then = (u + 1) * several // group
        for g in range(several):
            top = None
            if then is not None:
                at = (u + 1) * several + g
                q = jnp.concatenate([fqt[al(at * HEAD_DIM, HEAD_DIM), :], query_rows], axis=0)
            if now is not None:
                buf, x = now
                at = u * several + g
                rows = al(at * HEAD_DIM, HEAD_DIM)
                old = peak_in[pl.ds(at, 1), :]
                m = jnp.maximum(old, x[8 * g : 8 * g + 1, :])
                scaled = m * to_log2
                factor = jnp.exp2(old * to_log2 - scaled)
                peak[pl.ds(at, 1), :] = m
                t = total_in[pl.ds(at, 1), :] * factor
                a = accum_in[rows, :] * factor
            for b, (_, _, vref, vrow, _) in enumerate(shards):
                where = slice(g * span + b * tokens, g * span + (b + 1) * tokens)
                if then is not None:
                    k = keys[pl.ds(pl.multiple_of(h_then * span + b * tokens, tokens), tokens), :]
                    s = jnp.dot(k, q, preferred_element_type=f32)
                    then[0][where, :] = s
                    high = jnp.max(s.reshape(tokens // 8, 8, tokens), axis=0)
                    top = high if top is None else jnp.maximum(top, high)
                if now is not None:
                    p = jnp.exp2(buf[where, :] * to_log2 - scaled)
                    t = t + jnp.sum(p, axis=0, keepdims=True)
                    v = vref[pl.ds(pl.multiple_of(vrow + h * HEAD_DIM, PAD), HEAD_DIM), :]
                    a = a + jnp.dot(v, p.astype(bf16), preferred_element_type=f32)
            if then is not None:
                then[1][8 * g : 8 * g + 8, :] = column_peak(top)
            if now is not None:
                total[pl.ds(at, 1), :] = t
                accum[rows, :] = a

    two_deep(wide // HEAD_DIM // several, step, s0, s1, x0, x1)


def remote_scratch(kv, tokens, count):
    span = count * tokens
    several = 4 if count < 3 else 2
    return [
        pltpu.VMEM((kv * span, AUG), bf16),
        pltpu.VMEM((several * span, tokens), f32),
        pltpu.VMEM((several * span, tokens), f32),
        pltpu.VMEM((8 * several, tokens), f32),
        pltpu.VMEM((8 * several, tokens), f32),
    ]


def placed(shards, refs):
    return [(refs[ka], kr, refs[va], vr, flag) for ka, kr, va, vr, flag in shards]


def remote_kernel(group, shards, n, fqt, *refs):
    meta, peak_in, total_in, accum_in, peak, total, accum = refs[n : n + 7]
    remote_update(group, fqt, placed(shards, refs), meta, (peak_in, total_in, accum_in), (peak, total, accum), *refs[n + 7 :])


def remote(group, fqt, arrays, shards, meta, state):
    wide, tokens = fqt.shape
    heads = wide // HEAD_DIM
    count = len(shards)
    n = len(arrays)
    return pl.pallas_call(
        functools.partial(remote_kernel, group, shards, n),
        out_shape=tuple(jax.ShapeDtypeStruct(x.shape, x.dtype) for x in state),
        in_specs=[VM] * (n + 5),
        out_specs=(VM,) * 3,
        scratch_shapes=remote_scratch(heads // group, tokens, count),
        input_output_aliases={n + 2 + i: i for i in range(3)},
        compiler_params=pltpu.CompilerParams(vmem_limit_bytes=16 << 20),
        cost_estimate=pl.CostEstimate(
            flops=4 * wide * tokens * tokens * count * 4, transcendentals=heads * tokens * tokens * count, bytes_accessed=20 * wide * tokens
        ),
        name="remote",
    )(fqt, *arrays, meta, *state)


def last_kernel(group, shards, n, fqt, *refs):
    meta, peak_in, total_in, accum_in, held, mine, theirs = refs[n : n + 7]
    keys, s0, s1, x0, x1, peak, total, accum, mixed = refs[n + 7 :]
    remote_update(group, fqt, placed(shards, refs), meta, (peak_in, total_in, accum_in), (peak, total, accum), keys, s0, s1, x0, x1)
    wide, tokens = fqt.shape
    rows = tokens // 2
    for u in range(wide // HEAD_DIM):
        at = slice(u * HEAD_DIM, (u + 1) * HEAD_DIM)
        mixed[at, :] = (accum[at, :] / total[u : u + 1, :]).astype(bf16)
    first = meta[SIDE0 : SIDE0 + 1, :rows] > 0.0
    columns = held.shape[0]
    step = 4 * AUG
    for at in range(0, columns, step):
        size = min(step, columns - at)
        part = jnp.dot(held[at : at + size, :], mixed[...], preferred_element_type=f32).astype(bf16)
        low, high = part[:, :rows], part[:, rows:]
        mine[at : at + size, :] = jnp.where(first, low, high)
        theirs[at : at + size, :] = jnp.where(first, high, low)


def last(group, fqt, arrays, shards, meta, state, weight):
    wide, tokens = fqt.shape
    heads = wide // HEAD_DIM
    count = len(shards)
    n = len(arrays)
    return pl.pallas_call(
        functools.partial(last_kernel, group, shards, n),
        out_shape=(jax.ShapeDtypeStruct((weight.shape[0], tokens // 2), bf16),) * 2,
        in_specs=[VM] * (n + 6),
        out_specs=(VM, VM),
        scratch_shapes=remote_scratch(heads // group, tokens, count)
        + [
            pltpu.VMEM((heads, tokens), f32),
            pltpu.VMEM((heads, tokens), f32),
            pltpu.VMEM((wide, tokens), f32),
            pltpu.VMEM((wide, tokens), bf16),
        ],
        compiler_params=pltpu.CompilerParams(vmem_limit_bytes=28 << 20),
        cost_estimate=pl.CostEstimate(
            flops=4 * wide * tokens * tokens * count * 4, transcendentals=heads * tokens * tokens * count, bytes_accessed=20 * wide * tokens
        ),
        name="last",
    )(fqt, *arrays, meta, *state, weight)


def shifted_by(block, distance):
    size = lax.axis_size("ctx")
    return lax.ppermute(block, "ctx", [(i, (i + distance) % size) for i in range(size)])


def relayed(block):
    size = lax.axis_size("ctx")
    planes = size // PLANE
    target = {plane: plane + 2 for plane in range(1, planes - 2)}
    target.update({0: 0, planes - 1: 1, planes - 2: 2} if planes > 3 else {plane: plane for plane in range(planes)})
    return lax.ppermute(block, "ctx", [(i, target[i // PLANE] * PLANE + i % PLANE) for i in range(size)])


def swapped(block, bit):
    size = lax.axis_size("ctx")
    return lax.ppermute(block, "ctx", [(i, i ^ bit) for i in range(size)])


def body(banded_queries, banded_keys, banded_values, full_queries, full_keys, full_values, segment_ids, position_ids, out_weight):
    tokens = segment_ids.shape[0]
    width = full_keys.shape[1]
    height = 2 * width + PAD
    vrow = width + PAD
    group = banded_queries.shape[1] // banded_keys.shape[1]
    here = lax.axis_index("ctx")
    half = HEAD_DIM // 2
    frequency = theta_base ** (-2.0 * jnp.arange(half, dtype=f32) / HEAD_DIM)
    frequency = jnp.broadcast_to(frequency[:, None], (half, tokens))
    base = (here * tokens).astype(jnp.int32).reshape(1)
    side = lax.axis_index("head").astype(jnp.int32)

    kv = jnp.concatenate([full_keys, full_values, banded_keys, banded_values], axis=1)
    ids_pos = jnp.stack([segment_ids, position_ids])
    block, band_kv, rim, meta, cosine, sine = prepare(base, side.reshape(1), frequency, kv, ids_pos)
    z1 = shifted_by(block, PLANE)
    fqt, bqt, *state = own(group, full_queries, banded_queries, cosine, sine, block, meta)
    z1, rim, block, state = lax.optimization_barrier((z1, rim, block, state))

    rim = shifted_by(rim, 1)
    z3 = relayed(z1)
    z2 = shifted_by(z1, PLANE)
    x1 = swapped(z1, 1)
    y1 = swapped(z1, 2)
    state = remote(group, fqt, [z1], ((0, 0, 0, vrow, BACK + 1),), meta, state)
    rim, state = lax.optimization_barrier((rim, state))
    banded_out = band(group, bqt, band_kv, rim, meta)
    z2, z3, block, state, banded_out = lax.optimization_barrier((z2, z3, block, state, banded_out))

    def farthest(bit):
        return jnp.where((here & bit) == 0, block, z3)

    x2 = swapped(jnp.concatenate([z2, farthest(1)]), 1)
    y2 = swapped(jnp.concatenate([z2, farthest(2)]), 2)
    z2, z3, x1, y1 = lax.optimization_barrier((z2, z3, x1, y1))
    state = remote(group, fqt, [x1, y1, z2, z3], tuple((a, 0, a, vrow, flag) for a, flag in enumerate((BACK + 1, BACK + 1, BACK + 2, BACK + 3))), meta, state)
    x2, y2, state = lax.optimization_barrier((x2, y2, state))

    dx = swapped(jnp.concatenate([y1[:vrow], y2[height:]]), 1)
    dy = swapped(jnp.concatenate([x1[vrow:], x2[:height]]), 2)
    state = remote(
        group,
        fqt,
        [x2, y2],
        ((0, 0, 0, vrow, BACK + 2), (0, height, 0, height + vrow, PICK_X), (1, 0, 1, vrow, BACK + 2), (1, height, 1, height + vrow, PICK_Y)),
        meta,
        state,
    )
    dx, dy, state = lax.optimization_barrier((dx, dy, state))
    mine, theirs = last(
        group,
        fqt,
        [dx, dy],
        ((0, 0, 1, 0, BACK + 1), (0, vrow, 0, 2 * vrow, PICK_Y), (1, width, 1, width + vrow, BACK + 2)),
        meta,
        state,
        out_weight.T,
    )

    sides = lax.axis_size("head")
    if sides != 2:
        part = jnp.concatenate([jnp.where(side == 0, mine, theirs), jnp.where(side == 0, theirs, mine)], axis=1).T
        return banded_out, lax.psum_scatter(part, "head", scatter_dimension=0, tiled=True)
    theirs = lax.ppermute(theirs, "head", [(0, 1), (1, 0)])
    projected = (mine.astype(f32) + theirs.astype(f32)).astype(bf16)
    return banded_out, projected.T


def solution(mesh):
    return jax.shard_map(
        body,
        mesh=mesh,
        in_specs=(
            P("ctx", "head"),
            P("ctx", "head"),
            P("ctx", "head"),
            P("ctx", "head"),
            P("ctx", "head"),
            P("ctx", "head"),
            P("ctx"),
            P("ctx"),
            P("head", None),
        ),
        out_specs=(P("ctx", "head"), P(("ctx", "head"), None)),
        check_vma=False,
    )
```

profile of v0, /device:TPU:0, one launch (start us, length us, event | category | flops | bytes accessed | tf_op | source)
XLA Modules:
  0.0 76.7 jit_solution(14779756215665930584)
XLA Ops:
  0.6 0.0 copy-start.1
  0.7 0.8 %pad_add_fusion.ids_pos = s32[2,256]{1,0:T(2,128)S(1)} fusion(s32[1,256]{1,0:T(1,128)} %bitcast.10, s32[1,256]{1,0:T(1,128)} %bitcast.11), kind=kLoop, calls=%fused_computation.9 | loop fusion | flops 512 | bytes 4096 | tf_op jit(solution)/shard_map/stack | solution.py:494
  1.5 1.2 %pad_maximum_fusion.2.kv = bf16[256,1024]{1,0:T(8,128)(2,1)S(1)} fusion(bf16[256,256]{1,0:T(8,128)(2,1)} %param.11, bf16[256,256]{1,0:T(8,128)(2,1)} %param.10, bf16[256,256]{1,0:T(8,128)(2,1)} %param.14, bf16[256,256]{1,0:T(8,128)(2,1)} %param.13), kind=kLoop, calls=%fused_computation.4 | loop fusion | flops 2097152 | bytes 1048576 | tf_op jit(solution)/shard_map/concatenate | solution.py:493
  2.6 0.1 broadcast_in_dim.2.frequency
  2.7 0.4 prepare.1
  3.1 3.1 %collective-permute-start = (bf16[528,256]{1,0:T(8,128)(2,1)S(1)}, bf16[528,256]{1,0:T(8,128)(2,1)S(1)}, u32[]{:S(2)}, u32[]{:S(2)}) collective-permute-start(bf16[528,256]{1,0:T(8,128)(2,1)S(1)} %get-tuple-element.83.block), channel_id=1, source_target_pairs={{0,8},{2,10},{4,12},{6,14},{8,16},{10,18},{12,20},{14,22},{16,24},... | collective-permute-start | bytes 811016 | tf_op jit(solution)/shard_map/ppermute | solution.py:464
  6.2 0.0 copy-done.1
  6.2 0.0 copy-start.2
  6.2 1.2 %copy-done.2 = bf16[256,2048]{1,0:T(8,128)(2,1)S(1)} copy-done((bf16[256,2048]{1,0:T(8,128)(2,1)S(1)}, bf16[256,2048]{1,0:T(8,128)(2,1)}, u32[]{:S(2)}) %copy-start.2) | copy-done | bytes 1048600
  7.4 3.5 %own.1 = (bf16[2048,256]{1,0:T(8,128)(2,1)S(1)}, bf16[2048,256]{1,0:T(8,128)(2,1)S(1)}, f32[32,256]{1,0:T(8,128)S(1)}, f32[32,256]{1,0:T(8,128)S(1)}, f32[2048,256]{1,0:T(8,128)S(1)}) custom-call(bf16[256,2048]{1,0:T(8,128)(2,1)S(1)} %copy-done.1, bf16[256,2048]{1,0:T(8,128)(2,1)S(1)} %copy-done.2, f32[32,256]{1,0:T(8,128)S(1)} %get-tuple-element.57.cosine, ...), custom_call_target="tpu_custom_call" | custom-call | flops 2147483648 | bytes 6291456 | tf_op jit(solution)/shard_map/own/pallas_call | solution.py:206
  10.9 3.8 %collective-permute-done.refs_0_ = bf16[528,256]{1,0:T(8,128)(2,1)S(1)} collective-permute-done((bf16[528,256]{1,0:T(8,128)(2,1)S(1)}, bf16[528,256]{1,0:T(8,128)(2,1)S(1)}, u32[]{:S(2)}, u32[]{:S(2)}) %collective-permute-start) | collective-permute-done | bytes 270368 | tf_op jit(solution)/shard_map/ppermute | solution.py:464
  14.7 0.0 collective-permute-start.1
  14.7 0.7 collective-permute-start.2
  15.4 1.6 %collective-permute-start.4 = (bf16[528,256]{1,0:T(8,128)(2,1)S(1)}, bf16[528,256]{1,0:T(8,128)(2,1)S(1)}, u32[]{:S(2)}, u32[]{:S(2)}) collective-permute-start(bf16[528,256]{1,0:T(8,128)(2,1)S(1)} %collective-permute-done.refs_0_), channel_id=1, source_target_pairs={{0,2},{2,0},{4,6},{6,4},{8,10},{10,8},{12,14},{14,12},{16,18},{18,... | collective-permute-start | bytes 811016 | tf_op jit(solution)/shard_map/ppermute | solution.py:477
  16.9 1.5 %collective-permute-start.5 = (bf16[528,256]{1,0:T(8,128)(2,1)S(1)}, bf16[528,256]{1,0:T(8,128)(2,1)S(1)}, u32[]{:S(2)}, u32[]{:S(2)}) collective-permute-start(bf16[528,256]{1,0:T(8,128)(2,1)S(1)} %collective-permute-done.refs_0_), channel_id=1, source_target_pairs={{0,4},{2,6},{4,0},{6,2},{8,12},{10,14},{12,8},{14,10},{16,20},{18,... | collective-permute-start | bytes 811016 | tf_op jit(solution)/shard_map/ppermute | solution.py:477
  18.4 0.5 collective-permute-start.3
  19.0 3.0 %remote.3 = (f32[32,256]{1,0:T(8,128)S(1)}, f32[32,256]{1,0:T(8,128)S(1)}, f32[2048,256]{1,0:T(8,128)S(1)}) custom-call(bf16[2048,256]{1,0:T(8,128)(2,1)S(1)} %get-tuple-element.66.fqt, bf16[528,256]{1,0:T(8,128)(2,1)S(1)} %collective-permute-done.refs_0_, ...), custom_call_target="tpu_custom_call", output_to_operand_aliasing={{0}: (3, {}), {1}: (4, {}), {2}: (5, {})} | custom-call | flops 2147483648 | bytes 10485760 | tf_op jit(solution)/shard_map/remote/pallas_call | solution.py:402
  22.0 12.6 %collective-permute-done.3.rim = bf16[528,128]{1,0:T(8,128)(2,1)S(1)} collective-permute-done((bf16[528,128]{1,0:T(8,128)(2,1)S(1)}, bf16[528,128]{1,0:T(8,128)(2,1)S(1)}, u32[]{:S(2)}, u32[]{:S(2)}) %collective-permute-start.3) | collective-permute-done | bytes 135200 | tf_op jit(solution)/shard_map/ppermute | solution.py:464
  34.6 4.3 %band.1 = bf16[256,2048]{1,0:T(8,128)(2,1)} custom-call(bf16[2048,256]{1,0:T(8,128)(2,1)S(1)} %get-tuple-element.76.bqt, bf16[528,256]{1,0:T(8,128)(2,1)S(1)} %get-tuple-element.77.block, bf16[528,128]{1,0:T(8,128)(2,1)S(1)} %collective-permute-done.3.rim, f32[16,256]{1,0:T(8,128)S(1)} %get-tuple-element.59.meta.refs_1_.refs_4_.refs_2_), custom_call_target="tpu_custom_call" | custom-call | flops 2147483648 | bytes 2097152 | tf_op jit(solution)/shard_map/band/pallas_call | solution.py:294
  38.9 0.0 collective-permute-done.1.refs_2_
  38.9 0.0 collective-permute-done.2.refs_3_
  38.9 0.0 collective-permute-done.4.refs_0_
  38.9 0.0 collective-permute-done.5.refs_1_
  38.9 0.0 copy-start
  39.0 0.1 pad_maximum_fusion
  39.0 0.1 collective-permute-start.6
  39.1 0.1 collective-permute-start.7
  39.2 0.4 copy-done
  39.6 8.8 %remote.4 = (f32[32,256]{1,0:T(8,128)S(1)}, f32[32,256]{1,0:T(8,128)S(1)}, f32[2048,256]{1,0:T(8,128)S(1)}) custom-call(bf16[2048,256]{1,0:T(8,128)(2,1)S(1)} %get-tuple-element.66.fqt, bf16[528,256]{1,0:T(8,128)(2,1)S(1)} %collective-permute-done.4.refs_0_, ...), custom_call_target="tpu_custom_call", output_to_operand_aliasing={{0}: (6, {}), {1}: (7, {}), {2}: (8, {})} | custom-call | flops 8589934592 | bytes 10485760 | tf_op jit(solution)/shard_map/remote/pallas_call | solution.py:402
  48.4 0.0 slice-start
  48.4 2.7 %collective-permute-done.6.refs_0_ = bf16[1056,256]{1,0:T(8,128)(2,1)S(1)} collective-permute-done((bf16[1056,256]{1,0:T(8,128)(2,1)S(1)}, bf16[1056,256]{1,0:T(8,128)(2,1)S(1)}, u32[]{:S(2)}, u32[]{:S(2)}) %collective-permute-start.6) | collective-permute-done | bytes 540704 | tf_op jit(solution)/shard_map/ppermute | solution.py:477
  51.1 0.4 collective-permute-done.7.refs_1_
  51.6 0.1 collective-permute-start.9
  51.7 0.0 slice-done
  51.7 0.0 slice-start.1
  51.7 0.0 slice-start.2
  51.7 0.0 slice-start.3
  51.8 2.0 %collective-permute-start.8 = (bf16[800,256]{1,0:T(8,128)(2,1)S(1)}, bf16[800,256]{1,0:T(8,128)(2,1)S(1)}, u32[]{:S(2)}, u32[]{:S(2)}) collective-permute-start(bf16[800,256]{1,0:T(8,128)(2,1)S(1)} %pad_maximum_fusion.3), channel_id=1, source_target_pairs={{0,2},{2,0},{4,6},{6,4},{8,10},{10,8},{12,14},{14,12},{16,18},{18,... | collective-permute-start | bytes 1228808 | tf_op jit(solution)/shard_map/ppermute | solution.py:477
  53.8 8.7 %remote.5 = (f32[32,256]{1,0:T(8,128)S(1)}, f32[32,256]{1,0:T(8,128)S(1)}, f32[2048,256]{1,0:T(8,128)S(1)}) custom-call(bf16[2048,256]{1,0:T(8,128)(2,1)S(1)} %get-tuple-element.66.fqt, bf16[1056,256]{1,0:T(8,128)(2,1)S(1)} %collective-permute-done.6.refs_0_, ...), custom_call_target="tpu_custom_call", output_to_operand_aliasing={{0}: (4, {}), {1}: (5, {}), {2}: (6, {})} | custom-call | flops 8589934592 | bytes 10485760 | tf_op jit(solution)/shard_map/remote/pallas_call | solution.py:402
  62.5 0.0 collective-permute-done.9.refs_1_
  62.5 0.0 collective-permute-done.8.refs_0_
  62.5 0.0 slice-done.1
  62.6 0.0 slice-done.2
  62.6 0.0 slice-done.3
  62.6 10.8 %last.1 = (bf16[2880,128]{1,0:T(8,128)(2,1)S(1)}, bf16[2880,128]{1,0:T(8,128)(2,1)S(1)}) custom-call(bf16[2048,256]{1,0:T(8,128)(2,1)S(1)} %get-tuple-element.66.fqt, bf16[800,256]{1,0:T(8,128)(2,1)S(1)} %collective-permute-done.8.refs_0_, bf16[784,256]{1,0:T(8,128)(2,1)S(1)} %collective-permute-done.9.refs_1_, ...), custom_call_target="tpu_custom_call" | custom-call | flops 6442450944 | bytes 10485760 | tf_op jit(solution)/shard_map/last/pallas_call | solution.py:442
  73.4 0.1 collective-permute-start.10
  73.5 2.2 %collective-permute-done.10 = bf16[2880,128]{1,0:T(8,128)(2,1)S(1)} collective-permute-done((bf16[2880,128]{1,0:T(8,128)(2,1)S(1)}, bf16[2880,128]{1,0:T(8,128)(2,1)S(1)}, u32[]{:S(2)}, u32[]{:S(2)}) %collective-permute-start.10) | collective-permute-done | bytes 737312 | tf_op jit(solution)/shard_map/ppermute | solution.py:544
  75.7 1.1 %fusion = bf16[128,2880]{0,1:T(8,128)(2,1)} fusion(bf16[2880,128]{1,0:T(8,128)(2,1)S(1)} %collective-permute-done.10, bf16[2880,128]{1,0:T(8,128)(2,1)S(1)} %get-tuple-element.106), kind=kLoop, calls=%fused_computation.1 | loop fusion | flops 1474560 | bytes 2211840 | tf_op jit(solution)/shard_map/transpose | solution.py:546
  (8 shorter events, 0.2 us)
Async XLA Ops:
  0.6 5.5 %copy-start.1 = (bf16[256,2048]{1,0:T(8,128)(2,1)S(1)}, bf16[256,2048]{1,0:T(8,128)(2,1)}, u32[]{:S(2)}) copy-start(bf16[256,2048]{1,0:T(8,128)(2,1)} %fq.1) | copy-start | bytes 3145732
  3.1 11.6 %collective-permute-start = (bf16[528,256]{1,0:T(8,128)(2,1)S(1)}, bf16[528,256]{1,0:T(8,128)(2,1)S(1)}, u32[]{:S(2)}, u32[]{:S(2)}) collective-permute-start(bf16[528,256]{1,0:T(8,128)(2,1)S(1)} %get-tuple-element.83.block), channel_id=1, source_target_pairs={{0,8},{2,10},{4,12},{6,14},{8,16},{10,18},{12,20},{14,22},{16,24},... | collective-permute-start | bytes 811016 | tf_op jit(solution)/shard_map/ppermute | solution.py:464
  6.2 1.2 %copy-start.2 = (bf16[256,2048]{1,0:T(8,128)(2,1)S(1)}, bf16[256,2048]{1,0:T(8,128)(2,1)}, u32[]{:S(2)}) copy-start(bf16[256,2048]{1,0:T(8,128)(2,1)} %bq.1) | copy-start | bytes 3145732
  14.7 24.2 %collective-permute-start.1 = (bf16[528,256]{1,0:T(8,128)(2,1)S(1)}, bf16[528,256]{1,0:T(8,128)(2,1)S(1)}, u32[]{:S(2)}, u32[]{:S(2)}) collective-permute-start(bf16[528,256]{1,0:T(8,128)(2,1)S(1)} %collective-permute-done.refs_0_), channel_id=1, source_target_pairs={{0,8},{2,10},{4,12},{6,14},{8,16},{10,18},{12,20},{14,22},{16,24},... | collective-permute-start | bytes 811016 | tf_op jit(solution)/shard_map/ppermute | solution.py:464
  14.7 24.2 %collective-permute-start.2 = (bf16[528,256]{1,0:T(8,128)(2,1)S(1)}, bf16[528,256]{1,0:T(8,128)(2,1)S(1)}, u32[]{:S(2)}, u32[]{:S(2)}) collective-permute-start(bf16[528,256]{1,0:T(8,128)(2,1)S(1)} %collective-permute-done.refs_0_), channel_id=1, source_target_pairs={{0,0},{2,2},{4,4},{6,6},{8,24},{10,26},{12,28},{14,30},{16,16},{18... | collective-permute-start | bytes 811016 | tf_op jit(solution)/shard_map/ppermute | solution.py:472
  15.4 23.5 %collective-permute-start.4 = (bf16[528,256]{1,0:T(8,128)(2,1)S(1)}, bf16[528,256]{1,0:T(8,128)(2,1)S(1)}, u32[]{:S(2)}, u32[]{:S(2)}) collective-permute-start(bf16[528,256]{1,0:T(8,128)(2,1)S(1)} %collective-permute-done.refs_0_), channel_id=1, source_target_pairs={{0,2},{2,0},{4,6},{6,4},{8,10},{10,8},{12,14},{14,12},{16,18},{18,... | collective-permute-start | bytes 811016 | tf_op jit(solution)/shard_map/ppermute | solution.py:477
  16.9 22.0 %collective-permute-start.5 = (bf16[528,256]{1,0:T(8,128)(2,1)S(1)}, bf16[528,256]{1,0:T(8,128)(2,1)S(1)}, u32[]{:S(2)}, u32[]{:S(2)}) collective-permute-start(bf16[528,256]{1,0:T(8,128)(2,1)S(1)} %collective-permute-done.refs_0_), channel_id=1, source_target_pairs={{0,4},{2,6},{4,0},{6,2},{8,12},{10,14},{12,8},{14,10},{16,20},{18,... | collective-permute-start | bytes 811016 | tf_op jit(solution)/shard_map/ppermute | solution.py:477
  18.4 16.1 %collective-permute-start.3 = (bf16[528,128]{1,0:T(8,128)(2,1)S(1)}, bf16[528,128]{1,0:T(8,128)(2,1)S(1)}, u32[]{:S(2)}, u32[]{:S(2)}) collective-permute-start(bf16[528,128]{1,0:T(8,128)(2,1)S(1)} %get-tuple-element.65), channel_id=1, source_target_pairs={{0,2},{2,4},{4,6},{6,8},{8,10},{10,12},{12,14},{14,16},{16,18},{18... | collective-permute-start | bytes 405512 | tf_op jit(solution)/shard_map/ppermute | solution.py:464
  38.9 0.7 copy-start
  39.0 12.0 %collective-permute-start.6 = (bf16[1056,256]{1,0:T(8,128)(2,1)S(1)}, bf16[1056,256]{1,0:T(8,128)(2,1)S(1)}, u32[]{:S(2)}, u32[]{:S(2)}) collective-permute-start(bf16[1056,256]{1,0:T(8,128)(2,1)S(1)} %get-tuple-element.111), channel_id=1, source_target_pairs={{0,2},{2,0},{4,6},{6,4},{8,10},{10,8},{12,14},{14,12},{16,18},{18,... | collective-permute-start | bytes 1622024 | tf_op jit(solution)/shard_map/ppermute | solution.py:477
  39.1 12.4 %collective-permute-start.7 = (bf16[1056,256]{1,0:T(8,128)(2,1)S(1)}, bf16[1056,256]{1,0:T(8,128)(2,1)S(1)}, u32[]{:S(2)}, u32[]{:S(2)}) collective-permute-start(bf16[1056,256]{1,0:T(8,128)(2,1)S(1)} %get-tuple-element.110), channel_id=1, source_target_pairs={{0,4},{2,6},{4,0},{6,2},{8,12},{10,14},{12,8},{14,10},{16,20},{18,... | collective-permute-start | bytes 1622024 | tf_op jit(solution)/shard_map/ppermute | solution.py:477
  48.4 3.3 %slice-start = ((bf16[528,256]{1,0:T(8,128)(2,1)}), bf16[272,256]{1,0:T(8,128)(2,1)S(1)}, s32[]{:S(2)}) async-start(bf16[528,256]{1,0:T(8,128)(2,1)} %copy-done), calls=%async_computation | async-start | bytes 278528 | tf_op jit(solution)/shard_map/slice | solution.py:519
  51.6 11.0 %collective-permute-start.9 = (bf16[784,256]{1,0:T(8,128)(2,1)S(1)}, bf16[784,256]{1,0:T(8,128)(2,1)S(1)}, u32[]{:S(2)}, u32[]{:S(2)}) collective-permute-start(bf16[784,256]{1,0:T(8,128)(2,1)S(1)} %pad_maximum_fusion.4), channel_id=1, source_target_pairs={{0,4},{2,6},{4,0},{6,2},{8,12},{10,14},{12,8},{14,10},{16,20},{18,... | collective-permute-start | bytes 1204232 | tf_op jit(solution)/shard_map/ppermute | solution.py:477
  51.7 10.9 %slice-start.1 = ((s8[11796480]{0:T(1024)(128)(4,1)}), s8[4194304]{0:T(1024)(128)(4,1)S(1)}, s32[]{:S(2)}) async-start(s8[11796480]{0:T(1024)(128)(4,1)} %bitcast.7), calls=%async_computation.1 | async-start | bytes 8388608
  51.7 10.8 %slice-start.2 = ((s8[11796480]{0:T(1024)(128)(4,1)}), s8[4194304]{0:T(1024)(128)(4,1)S(1)}, s32[]{:S(2)}) async-start(s8[11796480]{0:T(1024)(128)(4,1)} %bitcast.7), calls=%async_computation.2 | async-start | bytes 8388608
  51.7 10.8 %slice-start.3 = ((s8[11796480]{0:T(1024)(128)(4,1)}), s8[3407872]{0:T(1024)(128)(4,1)S(1)}, s32[]{:S(2)}) async-start(s8[11796480]{0:T(1024)(128)(4,1)} %bitcast.7), calls=%async_computation.3 | async-start | bytes 6815744
  51.8 10.8 %collective-permute-start.8 = (bf16[800,256]{1,0:T(8,128)(2,1)S(1)}, bf16[800,256]{1,0:T(8,128)(2,1)S(1)}, u32[]{:S(2)}, u32[]{:S(2)}) collective-permute-start(bf16[800,256]{1,0:T(8,128)(2,1)S(1)} %pad_maximum_fusion.3), channel_id=1, source_target_pairs={{0,2},{2,0},{4,6},{6,4},{8,10},{10,8},{12,14},{14,12},{16,18},{18,... | collective-permute-start | bytes 1228808 | tf_op jit(solution)/shard_map/ppermute | solution.py:477
  73.4 2.3 %collective-permute-start.10 = (bf16[2880,128]{1,0:T(8,128)(2,1)S(1)}, bf16[2880,128]{1,0:T(8,128)(2,1)S(1)}, u32[]{:S(2)}, u32[]{:S(2)}) collective-permute-start(bf16[2880,128]{1,0:T(8,128)(2,1)S(1)} %get-tuple-element.107), channel_id=1, source_target_pairs={{0,1},{1,0},{2,3},{3,2},{4,5},{5,4},{6,7},{7,6},{8,9},{9,8},{10,11... | collective-permute-start | bytes 2211848 | tf_op jit(solution)/shard_map/ppermute | solution.py:544
where the time goes:
time: 76.9 us; the launch traced here: 76.7 us
  Pallas kernels  39.5 us (51%)
  waiting for transfers between devices  21.7 us (28%)
  starting transfers between devices  9.68 us (13%)
  other arithmetic  3.19 us (4%)
  local copies, waits for them, and re-layouts  1.76 us (2%)
  between operations  0.91 us (1%)
    pallas_call x3, Pallas kernels, remote(): pl.pallas_call(functools.partial(remote_kernel, group, shards, n), out_sh...  20.5 us
    ppermute x3, waiting for transfers between devices, shifted_by(): lax.ppermute(block, 'ctx', [(i, (i + distance) % size) for i in range(siz...  16.4 us
    pallas_call x1, Pallas kernels, last(): pl.pallas_call(functools.partial(last_kernel, group, shards, n), out_shap...  10.8 us
    ppermute x6, starting transfers between devices, swapped(): return lax.ppermute(block, 'ctx', [(i, i ^ bit) for i in range(size)])  5.3 us
    pallas_call x1, Pallas kernels, band(): pl.pallas_call(functools.partial(band_kernel, group), out_shape=jax.Shape...  4.3 us
    ppermute x3, starting transfers between devices, shifted_by(): lax.ppermute(block, 'ctx', [(i, (i + distance) % size) for i in range(siz...  3.64 us
    pallas_call x1, Pallas kernels, own(): pl.pallas_call(functools.partial(own_kernel, group), out_shape=(jax.Shape...  3.49 us
    ppermute x6, waiting for transfers between devices, swapped(): return lax.ppermute(block, 'ctx', [(i, i ^ bit) for i in range(size)])  3.11 us
  transfers between devices with their start and end apart: 11, of which 5 were waited for; matrix products, arithmetic and copies ran while one was open for 0% of the time, Pallas kernels for 37%

commit v1 on v0

--- a/solution.py
+++ b/solution.py
@@ -375,7 +375,7 @@
 
 def remote_scratch(kv, tokens, count):
     span = count * tokens
-    several = 4 if count < 3 else 2
+    several = 4
     return [
         pltpu.VMEM((kv * span, AUG), bf16),
         pltpu.VMEM((several * span, tokens), f32),
@@ -459,17 +459,10 @@
     )(fqt, *arrays, meta, *state, weight)
 
 
-def shifted_by(block, distance):
+def shifted_by(block, distance, first=None):
     size = lax.axis_size("ctx")
-    return lax.ppermute(block, "ctx", [(i, (i + distance) % size) for i in range(size)])
-
-
-def relayed(block):
-    size = lax.axis_size("ctx")
-    planes = size // PLANE
-    target = {plane: plane + 2 for plane in range(1, planes - 2)}
-    target.update({0: 0, planes - 1: 1, planes - 2: 2} if planes > 3 else {plane: plane for plane in range(planes)})
-    return lax.ppermute(block, "ctx", [(i, target[i // PLANE] * PLANE + i % PLANE) for i in range(size)])
+    route = [(i, (i + distance) % size) for i in range(size) if first is None or first <= i < size - distance]
+    return lax.ppermute(block, "ctx", route)
 
 
 def swapped(block, bit):
@@ -498,8 +491,8 @@
     z1, rim, block, state = lax.optimization_barrier((z1, rim, block, state))
 
     rim = shifted_by(rim, 1)
-    z3 = relayed(z1)
-    z2 = shifted_by(z1, PLANE)
+    z3 = shifted_by(z1, 2 * PLANE, PLANE)
+    z2 = shifted_by(z1, PLANE, PLANE)
     x1 = swapped(z1, 1)
     y1 = swapped(z1, 2)
     state = remote(group, fqt, [z1], ((0, 0, 0, vrow, BACK + 1),), meta, state)

time: 76.9 us -> 73.2 us (0.952)
  the two profiles are of different devices: /device:TPU:0 before, /device:TPU:24 now
where the time goes in v1:
time: 73.2 us; the launch traced here: 72.2 us
  Pallas kernels  37.9 us (52%)
  waiting for transfers between devices  19.9 us (27%)
  starting transfers between devices  8.54 us (12%)
  other arithmetic  3.19 us (4%)
  local copies, waits for them, and re-layouts  1.76 us (2%)
  between operations  0.95 us (1%)
    pallas_call x3, Pallas kernels, remote(): pl.pallas_call(functools.partial(remote_kernel, group, shards, n), out_sh...  20 us
    ppermute x4, waiting for transfers between devices, shifted_by(): return lax.ppermute(block, 'ctx', route)  14.2 us
    pallas_call x1, Pallas kernels, last(): pl.pallas_call(functools.partial(last_kernel, group, shards, n), out_shap...  9.74 us
    ppermute x6, starting transfers between devices, swapped(): return lax.ppermute(block, 'ctx', [(i, i ^ bit) for i in range(size)])  5.3 us
    pallas_call x1, Pallas kernels, band(): pl.pallas_call(functools.partial(band_kernel, group), out_shape=jax.Shape...  4.3 us
    pallas_call x1, Pallas kernels, own(): pl.pallas_call(functools.partial(own_kernel, group), out_shape=(jax.Shape...  3.49 us
    ppermute x6, waiting for transfers between devices, swapped(): return lax.ppermute(block, 'ctx', [(i, i ^ bit) for i in range(size)])  3.47 us
    ppermute x4, starting transfers between devices, shifted_by(): return lax.ppermute(block, 'ctx', route)  3.17 us
  transfers between devices with their start and end apart: 11, of which 5 were waited for; matrix products, arithmetic and copies ran while one was open for 0% of the time, Pallas kernels for 39%

profile of v1, /device:TPU:24, one launch (start us, length us, event | category | flops | bytes accessed | tf_op | source)
XLA Modules:
  0.0 72.2 jit_solution(9733990044920323591)
XLA Ops:
  0.6 0.0 copy-start.1
  0.7 0.8 %pad_add_fusion.ids_pos = s32[2,256]{1,0:T(2,128)S(1)} fusion(s32[1,256]{1,0:T(1,128)} %bitcast.10, s32[1,256]{1,0:T(1,128)} %bitcast.11), kind=kLoop, calls=%fused_computation.9 | loop fusion | flops 512 | bytes 4096 | tf_op jit(solution)/shard_map/stack | solution.py:487
  1.5 1.2 %pad_maximum_fusion.2.kv = bf16[256,1024]{1,0:T(8,128)(2,1)S(1)} fusion(bf16[256,256]{1,0:T(8,128)(2,1)} %param.11, bf16[256,256]{1,0:T(8,128)(2,1)} %param.10, bf16[256,256]{1,0:T(8,128)(2,1)} %param.14, bf16[256,256]{1,0:T(8,128)(2,1)} %param.13), kind=kLoop, calls=%fused_computation.4 | loop fusion | flops 2097152 | bytes 1048576 | tf_op jit(solution)/shard_map/concatenate | solution.py:486
  2.6 0.1 broadcast_in_dim.2.frequency
  2.7 0.4 prepare.1
  3.1 0.1 collective-permute-start
  3.1 0.0 copy-done.1
  3.2 0.0 copy-start.2
  3.2 1.2 %copy-done.2 = bf16[256,2048]{1,0:T(8,128)(2,1)S(1)} copy-done((bf16[256,2048]{1,0:T(8,128)(2,1)S(1)}, bf16[256,2048]{1,0:T(8,128)(2,1)}, u32[]{:S(2)}) %copy-start.2) | copy-done | bytes 1048600
  4.4 3.5 %own.1 = (bf16[2048,256]{1,0:T(8,128)(2,1)S(1)}, bf16[2048,256]{1,0:T(8,128)(2,1)S(1)}, f32[32,256]{1,0:T(8,128)S(1)}, f32[32,256]{1,0:T(8,128)S(1)}, f32[2048,256]{1,0:T(8,128)S(1)}) custom-call(bf16[256,2048]{1,0:T(8,128)(2,1)S(1)} %copy-done.1, bf16[256,2048]{1,0:T(8,128)(2,1)S(1)} %copy-done.2, f32[32,256]{1,0:T(8,128)S(1)} %get-tuple-element.57.cosine, ...), custom_call_target="tpu_custom_call" | custom-call | flops 2147483648 | bytes 6291456 | tf_op jit(solution)/shard_map/own/pallas_call | solution.py:206
  7.9 3.5 %collective-permute-done.refs_0_ = bf16[528,256]{1,0:T(8,128)(2,1)S(1)} collective-permute-done((bf16[528,256]{1,0:T(8,128)(2,1)S(1)}, bf16[528,256]{1,0:T(8,128)(2,1)S(1)}, u32[]{:S(2)}, u32[]{:S(2)}) %collective-permute-start) | collective-permute-done | bytes 270368 | tf_op jit(solution)/shard_map/ppermute | solution.py:465
  11.3 1.3 %collective-permute-start.1 = (bf16[528,256]{1,0:T(8,128)(2,1)S(1)}, bf16[528,256]{1,0:T(8,128)(2,1)S(1)}, u32[]{:S(2)}, u32[]{:S(2)}) collective-permute-start(bf16[528,256]{1,0:T(8,128)(2,1)S(1)} %collective-permute-done.refs_0_), channel_id=1, source_target_pairs={{8,16},{10,18},{12,20},{14,22},{16,24},{18,26},{20,28},{22,30},{9,... | collective-permute-start | bytes 811016 | tf_op jit(solution)/shard_map/ppermute | solution.py:465
  12.6 1.3 %collective-permute-start.2 = (bf16[528,256]{1,0:T(8,128)(2,1)S(1)}, bf16[528,256]{1,0:T(8,128)(2,1)S(1)}, u32[]{:S(2)}, u32[]{:S(2)}) collective-permute-start(bf16[528,256]{1,0:T(8,128)(2,1)S(1)} %collective-permute-done.refs_0_), channel_id=1, source_target_pairs={{8,24},{10,26},{12,28},{14,30},{9,25},{11,27},{13,29},{15,31}} | collective-permute-start | bytes 811016 | tf_op jit(solution)/shard_map/ppermute | solution.py:465
  13.9 1.6 %collective-permute-start.4 = (bf16[528,256]{1,0:T(8,128)(2,1)S(1)}, bf16[528,256]{1,0:T(8,128)(2,1)S(1)}, u32[]{:S(2)}, u32[]{:S(2)}) collective-permute-start(bf16[528,256]{1,0:T(8,128)(2,1)S(1)} %collective-permute-done.refs_0_), channel_id=1, source_target_pairs={{0,2},{2,0},{4,6},{6,4},{8,10},{10,8},{12,14},{14,12},{16,18},{18,... | collective-permute-start | bytes 811016 | tf_op jit(solution)/shard_map/ppermute | solution.py:470
  15.5 1.5 %collective-permute-start.5 = (bf16[528,256]{1,0:T(8,128)(2,1)S(1)}, bf16[528,256]{1,0:T(8,128)(2,1)S(1)}, u32[]{:S(2)}, u32[]{:S(2)}) collective-permute-start(bf16[528,256]{1,0:T(8,128)(2,1)S(1)} %collective-permute-done.refs_0_), channel_id=1, source_target_pairs={{0,4},{2,6},{4,0},{6,2},{8,12},{10,14},{12,8},{14,10},{16,20},{18,... | collective-permute-start | bytes 811016 | tf_op jit(solution)/shard_map/ppermute | solution.py:470
  17.0 0.5 collective-permute-start.3
  17.5 3.0 %remote.3 = (f32[32,256]{1,0:T(8,128)S(1)}, f32[32,256]{1,0:T(8,128)S(1)}, f32[2048,256]{1,0:T(8,128)S(1)}) custom-call(bf16[2048,256]{1,0:T(8,128)(2,1)S(1)} %get-tuple-element.66.fqt, bf16[528,256]{1,0:T(8,128)(2,1)S(1)} %collective-permute-done.refs_0_, ...), custom_call_target="tpu_custom_call", output_to_operand_aliasing={{0}: (3, {}), {1}: (4, {}), {2}: (5, {})} | custom-call | flops 2147483648 | bytes 10485760 | tf_op jit(solution)/shard_map/remote/pallas_call | solution.py:402
  20.5 10.7 %collective-permute-done.3.rim = bf16[528,128]{1,0:T(8,128)(2,1)S(1)} collective-permute-done((bf16[528,128]{1,0:T(8,128)(2,1)S(1)}, bf16[528,128]{1,0:T(8,128)(2,1)S(1)}, u32[]{:S(2)}, u32[]{:S(2)}) %collective-permute-start.3) | collective-permute-done | bytes 135200 | tf_op jit(solution)/shard_map/ppermute | solution.py:465
  31.3 4.3 %band.1 = bf16[256,2048]{1,0:T(8,128)(2,1)} custom-call(bf16[2048,256]{1,0:T(8,128)(2,1)S(1)} %get-tuple-element.76.bqt, bf16[528,256]{1,0:T(8,128)(2,1)S(1)} %get-tuple-element.77.block, bf16[528,128]{1,0:T(8,128)(2,1)S(1)} %collective-permute-done.3.rim, f32[16,256]{1,0:T(8,128)S(1)} %get-tuple-element.59.meta.refs_1_.refs_4_.refs_2_), custom_call_target="tpu_custom_call" | custom-call | flops 2147483648 | bytes 2097152 | tf_op jit(solution)/shard_map/band/pallas_call | solution.py:294
  35.6 0.0 collective-permute-done.1.refs_2_
  35.6 0.0 collective-permute-done.2.refs_3_
  35.6 0.0 collective-permute-done.4.refs_0_
  35.6 0.0 collective-permute-done.5.refs_1_
  35.6 0.0 copy-start
  35.7 0.1 pad_maximum_fusion
  35.7 0.1 collective-permute-start.6
  35.8 0.1 collective-permute-start.7
  35.9 0.4 copy-done
  36.3 8.4 %remote.4 = (f32[32,256]{1,0:T(8,128)S(1)}, f32[32,256]{1,0:T(8,128)S(1)}, f32[2048,256]{1,0:T(8,128)S(1)}) custom-call(bf16[2048,256]{1,0:T(8,128)(2,1)S(1)} %get-tuple-element.66.fqt, bf16[528,256]{1,0:T(8,128)(2,1)S(1)} %collective-permute-done.4.refs_0_, ...), custom_call_target="tpu_custom_call", output_to_operand_aliasing={{0}: (6, {}), {1}: (7, {}), {2}: (8, {})} | custom-call | flops 8589934592 | bytes 10485760 | tf_op jit(solution)/shard_map/remote/pallas_call | solution.py:402
  44.7 0.0 slice-start
  44.7 2.8 %collective-permute-done.6.refs_0_ = bf16[1056,256]{1,0:T(8,128)(2,1)S(1)} collective-permute-done((bf16[1056,256]{1,0:T(8,128)(2,1)S(1)}, bf16[1056,256]{1,0:T(8,128)(2,1)S(1)}, u32[]{:S(2)}, u32[]{:S(2)}) %collective-permute-start.6) | collective-permute-done | bytes 540704 | tf_op jit(solution)/shard_map/ppermute | solution.py:470
  47.6 0.6 collective-permute-done.7.refs_1_
  48.3 0.1 collective-permute-start.9
  48.4 0.0 slice-done
  48.4 0.0 slice-start.1
  48.4 0.0 slice-start.2
  48.4 0.0 slice-start.3
  48.4 2.0 %collective-permute-start.8 = (bf16[800,256]{1,0:T(8,128)(2,1)S(1)}, bf16[800,256]{1,0:T(8,128)(2,1)S(1)}, u32[]{:S(2)}, u32[]{:S(2)}) collective-permute-start(bf16[800,256]{1,0:T(8,128)(2,1)S(1)} %pad_maximum_fusion.3), channel_id=1, source_target_pairs={{0,2},{2,0},{4,6},{6,4},{8,10},{10,8},{12,14},{14,12},{16,18},{18,... | collective-permute-start | bytes 1228808 | tf_op jit(solution)/shard_map/ppermute | solution.py:470
  50.5 8.6 %remote.5 = (f32[32,256]{1,0:T(8,128)S(1)}, f32[32,256]{1,0:T(8,128)S(1)}, f32[2048,256]{1,0:T(8,128)S(1)}) custom-call(bf16[2048,256]{1,0:T(8,128)(2,1)S(1)} %get-tuple-element.66.fqt, bf16[1056,256]{1,0:T(8,128)(2,1)S(1)} %collective-permute-done.6.refs_0_, ...), custom_call_target="tpu_custom_call", output_to_operand_aliasing={{0}: (4, {}), {1}: (5, {}), {2}: (6, {})} | custom-call | flops 8589934592 | bytes 10485760 | tf_op jit(solution)/shard_map/remote/pallas_call | solution.py:402
  59.1 0.0 collective-permute-done.9.refs_1_
  59.1 0.0 collective-permute-done.8.refs_0_
  59.1 0.0 slice-done.1
  59.1 0.0 slice-done.2
  59.1 0.0 slice-done.3
  59.2 9.7 %last.1 = (bf16[2880,128]{1,0:T(8,128)(2,1)S(1)}, bf16[2880,128]{1,0:T(8,128)(2,1)S(1)}) custom-call(bf16[2048,256]{1,0:T(8,128)(2,1)S(1)} %get-tuple-element.66.fqt, bf16[800,256]{1,0:T(8,128)(2,1)S(1)} %collective-permute-done.8.refs_0_, bf16[784,256]{1,0:T(8,128)(2,1)S(1)} %collective-permute-done.9.refs_1_, ...), custom_call_target="tpu_custom_call" | custom-call | flops 6442450944 | bytes 10485760 | tf_op jit(solution)/shard_map/last/pallas_call | solution.py:442
  68.9 0.1 collective-permute-start.10
  69.0 2.2 %collective-permute-done.10 = bf16[2880,128]{1,0:T(8,128)(2,1)S(1)} collective-permute-done((bf16[2880,128]{1,0:T(8,128)(2,1)S(1)}, bf16[2880,128]{1,0:T(8,128)(2,1)S(1)}, u32[]{:S(2)}, u32[]{:S(2)}) %collective-permute-start.10) | collective-permute-done | bytes 737312 | tf_op jit(solution)/shard_map/ppermute | solution.py:537
  71.2 1.1 %fusion = bf16[128,2880]{0,1:T(8,128)(2,1)} fusion(bf16[2880,128]{1,0:T(8,128)(2,1)S(1)} %collective-permute-done.10, bf16[2880,128]{1,0:T(8,128)(2,1)S(1)} %get-tuple-element.106), kind=kLoop, calls=%fused_computation.1 | loop fusion | flops 1474560 | bytes 2211840 | tf_op jit(solution)/shard_map/transpose | solution.py:539
  (8 shorter events, 0.2 us)
Async XLA Ops:
  0.6 2.5 %copy-start.1 = (bf16[256,2048]{1,0:T(8,128)(2,1)S(1)}, bf16[256,2048]{1,0:T(8,128)(2,1)}, u32[]{:S(2)}) copy-start(bf16[256,2048]{1,0:T(8,128)(2,1)} %fq.1) | copy-start | bytes 3145732
  3.1 8.3 %collective-permute-start = (bf16[528,256]{1,0:T(8,128)(2,1)S(1)}, bf16[528,256]{1,0:T(8,128)(2,1)S(1)}, u32[]{:S(2)}, u32[]{:S(2)}) collective-permute-start(bf16[528,256]{1,0:T(8,128)(2,1)S(1)} %get-tuple-element.83.block), channel_id=1, source_target_pairs={{0,8},{2,10},{4,12},{6,14},{8,16},{10,18},{12,20},{14,22},{16,24},... | collective-permute-start | bytes 811016 | tf_op jit(solution)/shard_map/ppermute | solution.py:465
  3.2 1.2 %copy-start.2 = (bf16[256,2048]{1,0:T(8,128)(2,1)S(1)}, bf16[256,2048]{1,0:T(8,128)(2,1)}, u32[]{:S(2)}) copy-start(bf16[256,2048]{1,0:T(8,128)(2,1)} %bq.1) | copy-start | bytes 3145732
  11.3 24.2 %collective-permute-start.1 = (bf16[528,256]{1,0:T(8,128)(2,1)S(1)}, bf16[528,256]{1,0:T(8,128)(2,1)S(1)}, u32[]{:S(2)}, u32[]{:S(2)}) collective-permute-start(bf16[528,256]{1,0:T(8,128)(2,1)S(1)} %collective-permute-done.refs_0_), channel_id=1, source_target_pairs={{8,16},{10,18},{12,20},{14,22},{16,24},{18,26},{20,28},{22,30},{9,... | collective-permute-start | bytes 811016 | tf_op jit(solution)/shard_map/ppermute | solution.py:465
  12.6 22.9 %collective-permute-start.2 = (bf16[528,256]{1,0:T(8,128)(2,1)S(1)}, bf16[528,256]{1,0:T(8,128)(2,1)S(1)}, u32[]{:S(2)}, u32[]{:S(2)}) collective-permute-start(bf16[528,256]{1,0:T(8,128)(2,1)S(1)} %collective-permute-done.refs_0_), channel_id=1, source_target_pairs={{8,24},{10,26},{12,28},{14,30},{9,25},{11,27},{13,29},{15,31}} | collective-permute-start | bytes 811016 | tf_op jit(solution)/shard_map/ppermute | solution.py:465
  13.9 21.6 %collective-permute-start.4 = (bf16[528,256]{1,0:T(8,128)(2,1)S(1)}, bf16[528,256]{1,0:T(8,128)(2,1)S(1)}, u32[]{:S(2)}, u32[]{:S(2)}) collective-permute-start(bf16[528,256]{1,0:T(8,128)(2,1)S(1)} %collective-permute-done.refs_0_), channel_id=1, source_target_pairs={{0,2},{2,0},{4,6},{6,4},{8,10},{10,8},{12,14},{14,12},{16,18},{18,... | collective-permute-start | bytes 811016 | tf_op jit(solution)/shard_map/ppermute | solution.py:470
  15.5 20.1 %collective-permute-start.5 = (bf16[528,256]{1,0:T(8,128)(2,1)S(1)}, bf16[528,256]{1,0:T(8,128)(2,1)S(1)}, u32[]{:S(2)}, u32[]{:S(2)}) collective-permute-start(bf16[528,256]{1,0:T(8,128)(2,1)S(1)} %collective-permute-done.refs_0_), channel_id=1, source_target_pairs={{0,4},{2,6},{4,0},{6,2},{8,12},{10,14},{12,8},{14,10},{16,20},{18,... | collective-permute-start | bytes 811016 | tf_op jit(solution)/shard_map/ppermute | solution.py:470
  17.0 14.3 %collective-permute-start.3 = (bf16[528,128]{1,0:T(8,128)(2,1)S(1)}, bf16[528,128]{1,0:T(8,128)(2,1)S(1)}, u32[]{:S(2)}, u32[]{:S(2)}) collective-permute-start(bf16[528,128]{1,0:T(8,128)(2,1)S(1)} %get-tuple-element.65), channel_id=1, source_target_pairs={{0,2},{2,4},{4,6},{6,8},{8,10},{10,12},{12,14},{14,16},{16,18},{18... | collective-permute-start | bytes 405512 | tf_op jit(solution)/shard_map/ppermute | solution.py:465
  35.6 0.7 copy-start
  35.7 11.8 %collective-permute-start.6 = (bf16[1056,256]{1,0:T(8,128)(2,1)S(1)}, bf16[1056,256]{1,0:T(8,128)(2,1)S(1)}, u32[]{:S(2)}, u32[]{:S(2)}) collective-permute-start(bf16[1056,256]{1,0:T(8,128)(2,1)S(1)} %get-tuple-element.111), channel_id=1, source_target_pairs={{0,2},{2,0},{4,6},{6,4},{8,10},{10,8},{12,14},{14,12},{16,18},{18,... | collective-permute-start | bytes 1622024 | tf_op jit(solution)/shard_map/ppermute | solution.py:470
  35.8 12.4 %collective-permute-start.7 = (bf16[1056,256]{1,0:T(8,128)(2,1)S(1)}, bf16[1056,256]{1,0:T(8,128)(2,1)S(1)}, u32[]{:S(2)}, u32[]{:S(2)}) collective-permute-start(bf16[1056,256]{1,0:T(8,128)(2,1)S(1)} %get-tuple-element.110), channel_id=1, source_target_pairs={{0,4},{2,6},{4,0},{6,2},{8,12},{10,14},{12,8},{14,10},{16,20},{18,... | collective-permute-start | bytes 1622024 | tf_op jit(solution)/shard_map/ppermute | solution.py:470
  44.7 3.6 %slice-start = ((bf16[528,256]{1,0:T(8,128)(2,1)}), bf16[272,256]{1,0:T(8,128)(2,1)S(1)}, s32[]{:S(2)}) async-start(bf16[528,256]{1,0:T(8,128)(2,1)} %copy-done), calls=%async_computation | async-start | bytes 278528 | tf_op jit(solution)/shard_map/slice | solution.py:512
  48.3 10.9 %collective-permute-start.9 = (bf16[784,256]{1,0:T(8,128)(2,1)S(1)}, bf16[784,256]{1,0:T(8,128)(2,1)S(1)}, u32[]{:S(2)}, u32[]{:S(2)}) collective-permute-start(bf16[784,256]{1,0:T(8,128)(2,1)S(1)} %pad_maximum_fusion.4), channel_id=1, source_target_pairs={{0,4},{2,6},{4,0},{6,2},{8,12},{10,14},{12,8},{14,10},{16,20},{18,... | collective-permute-start | bytes 1204232 | tf_op jit(solution)/shard_map/ppermute | solution.py:470
  48.4 10.8 %slice-start.1 = ((s8[11796480]{0:T(1024)(128)(4,1)}), s8[4194304]{0:T(1024)(128)(4,1)S(1)}, s32[]{:S(2)}) async-start(s8[11796480]{0:T(1024)(128)(4,1)} %bitcast.7), calls=%async_computation.1 | async-start | bytes 8388608
  48.4 10.7 %slice-start.2 = ((s8[11796480]{0:T(1024)(128)(4,1)}), s8[4194304]{0:T(1024)(128)(4,1)S(1)}, s32[]{:S(2)}) async-start(s8[11796480]{0:T(1024)(128)(4,1)} %bitcast.7), calls=%async_computation.2 | async-start | bytes 8388608
  48.4 10.7 %slice-start.3 = ((s8[11796480]{0:T(1024)(128)(4,1)}), s8[3407872]{0:T(1024)(128)(4,1)S(1)}, s32[]{:S(2)}) async-start(s8[11796480]{0:T(1024)(128)(4,1)} %bitcast.7), calls=%async_computation.3 | async-start | bytes 6815744
  48.4 10.7 %collective-permute-start.8 = (bf16[800,256]{1,0:T(8,128)(2,1)S(1)}, bf16[800,256]{1,0:T(8,128)(2,1)S(1)}, u32[]{:S(2)}, u32[]{:S(2)}) collective-permute-start(bf16[800,256]{1,0:T(8,128)(2,1)S(1)} %pad_maximum_fusion.3), channel_id=1, source_target_pairs={{0,2},{2,0},{4,6},{6,4},{8,10},{10,8},{12,14},{14,12},{16,18},{18,... | collective-permute-start | bytes 1228808 | tf_op jit(solution)/shard_map/ppermute | solution.py:470
  68.9 2.3 %collective-permute-start.10 = (bf16[2880,128]{1,0:T(8,128)(2,1)S(1)}, bf16[2880,128]{1,0:T(8,128)(2,1)S(1)}, u32[]{:S(2)}, u32[]{:S(2)}) collective-permute-start(bf16[2880,128]{1,0:T(8,128)(2,1)S(1)} %get-tuple-element.107), channel_id=1, source_target_pairs={{0,1},{1,0},{2,3},{3,2},{4,5},{5,4},{6,7},{7,6},{8,9},{9,8},{10,11... | collective-permute-start | bytes 2211848 | tf_op jit(solution)/shard_map/ppermute | solution.py:537

commit v2 on v1

--- a/solution.py
+++ b/solution.py
@@ -495,18 +495,17 @@
     z2 = shifted_by(z1, PLANE, PLANE)
     x1 = swapped(z1, 1)
     y1 = swapped(z1, 2)
-    state = remote(group, fqt, [z1], ((0, 0, 0, vrow, BACK + 1),), meta, state)
-    rim, state = lax.optimization_barrier((rim, state))
     banded_out = band(group, bqt, band_kv, rim, meta)
-    z2, z3, block, state, banded_out = lax.optimization_barrier((z2, z3, block, state, banded_out))
+    z2, z3, block, banded_out = lax.optimization_barrier((z2, z3, block, banded_out))
 
     def farthest(bit):
         return jnp.where((here & bit) == 0, block, z3)
 
     x2 = swapped(jnp.concatenate([z2, farthest(1)]), 1)
     y2 = swapped(jnp.concatenate([z2, farthest(2)]), 2)
-    z2, z3, x1, y1 = lax.optimization_barrier((z2, z3, x1, y1))
-    state = remote(group, fqt, [x1, y1, z2, z3], tuple((a, 0, a, vrow, flag) for a, flag in enumerate((BACK + 1, BACK + 1, BACK + 2, BACK + 3))), meta, state)
+    z1, z2, z3, x1, y1 = lax.optimization_barrier((z1, z2, z3, x1, y1))
+    back = (BACK + 1, BACK + 1, BACK + 1, BACK + 2, BACK + 3)
+    state = remote(group, fqt, [z1, x1, y1, z2, z3], tuple((a, 0, a, vrow, flag) for a, flag in enumerate(back)), meta, state)
     x2, y2, state = lax.optimization_barrier((x2, y2, state))
 
     dx = swapped(jnp.concatenate([y1[:vrow], y2[height:]]), 1)

time: 73.2 us -> 67.4 us (0.921)
  waiting for transfers between devices: 19.9 us -> 9.23 us
  starting transfers between devices: 8.54 us -> 12.9 us
  local copies, waits for them, and re-layouts: 1.76 us -> 3.72 us
  Pallas kernels: 37.9 us -> 36.7 us
    ppermute x4, waiting for transfers between devices: 14.2 us -> 6.18 us  [shifted_by(): return lax.ppermute(block, 'ctx', route)]
    ppermute x6, starting transfers between devices: 5.3 us -> 8.71 us  [swapped(): return lax.ppermute(block, 'ctx', [(i, i ^ bit) for i in range(size)])]
    ppermute x6, waiting for transfers between devices: 3.47 us -> 0.85 us  [swapped(): return lax.ppermute(block, 'ctx', [(i, i ^ bit) for i in range(size)])]
    unnamed x12 -> x20, local copies, waits for them, and re-layouts: 1.63 us -> 3.6 us
    pallas_call x3 -> x2, Pallas kernels: 20 us -> 18.4 us  [remote(): pl.pallas_call(functools.partial(remote_kernel, group, shards, n), out_sh...]
    ppermute x4, starting transfers between devices: 3.17 us -> 4.12 us  [shifted_by(): return lax.ppermute(block, 'ctx', route)]
  transfers between devices with their start and end apart: 11 -> 11, of which waited for: 5 -> 4; matrix products, arithmetic and copies ran while one was open for 0% -> 0% of each run, Pallas kernels for 39% -> 40%
where the time goes in v2:
time: 67.4 us; the launch traced here: 66.7 us
  Pallas kernels  36.7 us (54%)
  starting transfers between devices  12.9 us (19%)
  waiting for transfers between devices  9.23 us (14%)
  local copies, waits for them, and re-layouts  3.72 us (6%)
  other arithmetic  3.19 us (5%)
  between operations  0.94 us (1%)
    pallas_call x2, Pallas kernels, remote(): pl.pallas_call(functools.partial(remote_kernel, group, shards, n), out_sh...  18.4 us
    pallas_call x1, Pallas kernels, last(): pl.pallas_call(functools.partial(last_kernel, group, shards, n), out_shap...  9.95 us
    ppermute x6, starting transfers between devices, swapped(): return lax.ppermute(block, 'ctx', [(i, i ^ bit) for i in range(size)])  8.71 us
    ppermute x4, waiting for transfers between devices, shifted_by(): return lax.ppermute(block, 'ctx', route)  6.18 us
    pallas_call x1, Pallas kernels, band(): pl.pallas_call(functools.partial(band_kernel, group), out_shape=jax.Shape...  4.43 us
    ppermute x4, starting transfers between devices, shifted_by(): return lax.ppermute(block, 'ctx', route)  4.12 us
    unnamed x20, local copies, waits for them, and re-layouts  3.6 us
    pallas_call x1, Pallas kernels, own(): pl.pallas_call(functools.partial(own_kernel, group), out_shape=(jax.Shape...  3.52 us
  transfers between devices with their start and end apart: 11, of which 4 were waited for; matrix products, arithmetic and copies ran while one was open for 0% of the time, Pallas kernels for 40%

profile of v2, /device:TPU:24, one launch (start us, length us, event | category | flops | bytes accessed | tf_op | source)
XLA Modules:
  0.0 66.7 jit_solution(9929739440678169596)
XLA Ops:
  0.6 0.0 copy-start.1
  0.7 0.8 %pad_add_fusion.ids_pos = s32[2,256]{1,0:T(2,128)S(1)} fusion(s32[1,256]{1,0:T(1,128)} %bitcast.10, s32[1,256]{1,0:T(1,128)} %bitcast.11), kind=kLoop, calls=%fused_computation.9 | loop fusion | flops 512 | bytes 4096 | tf_op jit(solution)/shard_map/stack | solution.py:487
  1.5 1.2 %pad_maximum_fusion.2.kv = bf16[256,1024]{1,0:T(8,128)(2,1)S(1)} fusion(bf16[256,256]{1,0:T(8,128)(2,1)} %param.11, bf16[256,256]{1,0:T(8,128)(2,1)} %param.10, bf16[256,256]{1,0:T(8,128)(2,1)} %param.14, bf16[256,256]{1,0:T(8,128)(2,1)} %param.13), kind=kLoop, calls=%fused_computation.4 | loop fusion | flops 2097152 | bytes 1048576 | tf_op jit(solution)/shard_map/concatenate | solution.py:486
  2.6 0.1 broadcast_in_dim.2.frequency
  2.7 0.4 prepare.1
  3.1 0.1 collective-permute-start
  3.1 0.0 copy-done.1
  3.1 0.0 copy-start.2
  3.2 1.2 %copy-done.2 = bf16[256,2048]{1,0:T(8,128)(2,1)S(1)} copy-done((bf16[256,2048]{1,0:T(8,128)(2,1)S(1)}, bf16[256,2048]{1,0:T(8,128)(2,1)}, u32[]{:S(2)}) %copy-start.2) | copy-done | bytes 1048600
  4.4 3.5 %own.1 = (bf16[2048,256]{1,0:T(8,128)(2,1)S(1)}, bf16[2048,256]{1,0:T(8,128)(2,1)S(1)}, f32[32,256]{1,0:T(8,128)S(1)}, f32[32,256]{1,0:T(8,128)S(1)}, f32[2048,256]{1,0:T(8,128)S(1)}) custom-call(bf16[256,2048]{1,0:T(8,128)(2,1)S(1)} %copy-done.1, bf16[256,2048]{1,0:T(8,128)(2,1)S(1)} %copy-done.2, f32[32,256]{1,0:T(8,128)S(1)} %get-tuple-element.48.cosine, ...), custom_call_target="tpu_custom_call" | custom-call | flops 2147483648 | bytes 6291456 | tf_op jit(solution)/shard_map/own/pallas_call | solution.py:206
  7.9 0.0 copy-start.3
  7.9 1.4 %copy-done.3 = f32[2048,256]{1,0:T(8,128)} copy-done((f32[2048,256]{1,0:T(8,128)}, f32[2048,256]{1,0:T(8,128)S(1)}, u32[]{:S(2)}) %copy-start.3) | copy-done | bytes 2097176
  9.3 0.0 copy-start.5
  9.3 1.0 %copy-done.5 = bf16[2048,256]{1,0:T(8,128)(2,1)} copy-done((bf16[2048,256]{1,0:T(8,128)(2,1)}, bf16[2048,256]{1,0:T(8,128)(2,1)S(1)}, u32[]{:S(2)}) %copy-start.5) | copy-done | bytes 1048600
  10.3 1.1 %collective-permute-done.refs_0_ = bf16[528,256]{1,0:T(8,128)(2,1)S(1)} collective-permute-done((bf16[528,256]{1,0:T(8,128)(2,1)S(1)}, bf16[528,256]{1,0:T(8,128)(2,1)S(1)}, u32[]{:S(2)}, u32[]{:S(2)}) %collective-permute-start) | collective-permute-done | bytes 270368 | tf_op jit(solution)/shard_map/ppermute | solution.py:465
  11.3 1.5 %collective-permute-start.3 = (bf16[528,128]{1,0:T(8,128)(2,1)S(1)}, bf16[528,128]{1,0:T(8,128)(2,1)S(1)}, u32[]{:S(2)}, u32[]{:S(2)}) collective-permute-start(bf16[528,128]{1,0:T(8,128)(2,1)S(1)} %get-tuple-element.58), channel_id=1, source_target_pairs={{0,2},{2,4},{4,6},{6,8},{8,10},{10,12},{12,14},{14,16},{16,18},{18... | collective-permute-start | bytes 405512 | tf_op jit(solution)/shard_map/ppermute | solution.py:465
  12.8 1.3 %collective-permute-start.1 = (bf16[528,256]{1,0:T(8,128)(2,1)S(1)}, bf16[528,256]{1,0:T(8,128)(2,1)S(1)}, u32[]{:S(2)}, u32[]{:S(2)}) collective-permute-start(bf16[528,256]{1,0:T(8,128)(2,1)S(1)} %collective-permute-done.refs_0_), channel_id=1, source_target_pairs={{8,16},{10,18},{12,20},{14,22},{16,24},{18,26},{20,28},{22,30},{9,... | collective-permute-start | bytes 811016 | tf_op jit(solution)/shard_map/ppermute | solution.py:465
  14.1 1.3 %collective-permute-start.2 = (bf16[528,256]{1,0:T(8,128)(2,1)S(1)}, bf16[528,256]{1,0:T(8,128)(2,1)S(1)}, u32[]{:S(2)}, u32[]{:S(2)}) collective-permute-start(bf16[528,256]{1,0:T(8,128)(2,1)S(1)} %collective-permute-done.refs_0_), channel_id=1, source_target_pairs={{8,24},{10,26},{12,28},{14,30},{9,25},{11,27},{13,29},{15,31}} | collective-permute-start | bytes 811016 | tf_op jit(solution)/shard_map/ppermute | solution.py:465
  15.4 1.6 %collective-permute-start.4 = (bf16[528,256]{1,0:T(8,128)(2,1)S(1)}, bf16[528,256]{1,0:T(8,128)(2,1)S(1)}, u32[]{:S(2)}, u32[]{:S(2)}) collective-permute-start(bf16[528,256]{1,0:T(8,128)(2,1)S(1)} %collective-permute-done.refs_0_), channel_id=1, source_target_pairs={{0,2},{2,0},{4,6},{6,4},{8,10},{10,8},{12,14},{14,12},{16,18},{18,... | collective-permute-start | bytes 811016 | tf_op jit(solution)/shard_map/ppermute | solution.py:470
  17.0 2.0 %collective-permute-start.5 = (bf16[528,256]{1,0:T(8,128)(2,1)S(1)}, bf16[528,256]{1,0:T(8,128)(2,1)S(1)}, u32[]{:S(2)}, u32[]{:S(2)}) collective-permute-start(bf16[528,256]{1,0:T(8,128)(2,1)S(1)} %collective-permute-done.refs_0_), channel_id=1, source_target_pairs={{0,4},{2,6},{4,0},{6,2},{8,12},{10,14},{12,8},{14,10},{16,20},{18,... | collective-permute-start | bytes 811016 | tf_op jit(solution)/shard_map/ppermute | solution.py:470
  19.0 0.0 collective-permute-done.3.rim
  19.0 4.4 %band.1 = bf16[256,2048]{1,0:T(8,128)(2,1)} custom-call(bf16[2048,256]{1,0:T(8,128)(2,1)S(1)} %get-tuple-element.56.bqt, bf16[528,256]{1,0:T(8,128)(2,1)S(1)} %get-tuple-element.57.block, bf16[528,128]{1,0:T(8,128)(2,1)S(1)} %collective-permute-done.3.rim, f32[16,256]{1,0:T(8,128)S(1)} %get-tuple-element.50.meta.refs_5_.refs_2_), custom_call_target="tpu_custom_call" | custom-call | flops 2147483648 | bytes 2097152 | tf_op jit(solution)/shard_map/band/pallas_call | solution.py:294
  23.4 0.0 collective-permute-done.1.refs_3_
  23.4 5.1 %collective-permute-done.2.refs_4_ = bf16[528,256]{1,0:T(8,128)(2,1)S(1)} collective-permute-done((bf16[528,256]{1,0:T(8,128)(2,1)S(1)}, bf16[528,256]{1,0:T(8,128)(2,1)S(1)}, u32[]{:S(2)}, u32[]{:S(2)}) %collective-permute-start.2) | collective-permute-done | bytes 270368 | tf_op jit(solution)/shard_map/ppermute | solution.py:465
  28.5 0.0 collective-permute-done.4.refs_1_
  28.5 0.0 collective-permute-done.5.refs_2_
  28.5 0.0 copy-start
  28.5 0.0 copy-start.6
  28.5 0.1 broadcast_select_fusion
  28.6 0.0 copy-start.4
  28.6 0.1 pad_maximum_fusion
  28.7 1.6 %collective-permute-start.6 = (bf16[1056,256]{1,0:T(8,128)(2,1)S(1)}, bf16[1056,256]{1,0:T(8,128)(2,1)S(1)}, u32[]{:S(2)}, u32[]{:S(2)}) collective-permute-start(bf16[1056,256]{1,0:T(8,128)(2,1)S(1)} %get-tuple-element.93), channel_id=1, source_target_pairs={{0,2},{2,0},{4,6},{6,4},{8,10},{10,8},{12,14},{14,12},{16,18},{18,... | collective-permute-start | bytes 1622024 | tf_op jit(solution)/shard_map/ppermute | solution.py:470
  30.2 1.4 %collective-permute-start.7 = (bf16[1056,256]{1,0:T(8,128)(2,1)S(1)}, bf16[1056,256]{1,0:T(8,128)(2,1)S(1)}, u32[]{:S(2)}, u32[]{:S(2)}) collective-permute-start(bf16[1056,256]{1,0:T(8,128)(2,1)S(1)} %get-tuple-element.92), channel_id=1, source_target_pairs={{0,4},{2,6},{4,0},{6,2},{8,12},{10,14},{12,8},{14,10},{16,20},{18,... | collective-permute-start | bytes 1622024 | tf_op jit(solution)/shard_map/ppermute | solution.py:470
  31.7 0.0 copy-done
  31.7 0.0 copy-done.6
  31.7 0.0 copy-done.4
  31.7 10.0 %remote.2 = (f32[32,256]{1,0:T(8,128)S(1)}, f32[32,256]{1,0:T(8,128)S(1)}, f32[2048,256]{1,0:T(8,128)S(1)}) custom-call(bf16[2048,256]{1,0:T(8,128)(2,1)S(1)} %copy-done.6, bf16[528,256]{1,0:T(8,128)(2,1)S(1)} %collective-permute-done.refs_0_, ...), custom_call_target="tpu_custom_call", output_to_operand_aliasing={{0}: (7, {}), {1}: (8, {}), {2}: (9, {})} | custom-call | flops 10737418240 | bytes 10485760 | tf_op jit(solution)/shard_map/remote/pallas_call | solution.py:402
  41.7 0.0 slice-start
  41.7 0.0 collective-permute-done.6.refs_0_
  41.7 0.8 %collective-permute-done.7.refs_1_ = bf16[1056,256]{1,0:T(8,128)(2,1)S(1)} collective-permute-done((bf16[1056,256]{1,0:T(8,128)(2,1)S(1)}, bf16[1056,256]{1,0:T(8,128)(2,1)S(1)}, u32[]{:S(2)}, u32[]{:S(2)}) %collective-permute-start.7) | collective-permute-done | bytes 540704 | tf_op jit(solution)/shard_map/ppermute | solution.py:470
  42.6 1.5 %collective-permute-start.9 = (bf16[784,256]{1,0:T(8,128)(2,1)S(1)}, bf16[784,256]{1,0:T(8,128)(2,1)S(1)}, u32[]{:S(2)}, u32[]{:S(2)}) collective-permute-start(bf16[784,256]{1,0:T(8,128)(2,1)S(1)} %pad_maximum_fusion.4), channel_id=1, source_target_pairs={{0,4},{2,6},{4,0},{6,2},{8,12},{10,14},{12,8},{14,10},{16,20},{18,... | collective-permute-start | bytes 1204232 | tf_op jit(solution)/shard_map/ppermute | solution.py:470
  44.2 0.0 slice-done
  44.2 0.0 slice-start.1
  44.2 0.0 slice-start.2
  44.3 0.0 slice-start.3
  44.3 0.6 collective-permute-start.8
  44.9 8.4 %remote.3 = (f32[32,256]{1,0:T(8,128)S(1)}, f32[32,256]{1,0:T(8,128)S(1)}, f32[2048,256]{1,0:T(8,128)S(1)}) custom-call(bf16[2048,256]{1,0:T(8,128)(2,1)S(1)} %copy-done.6, bf16[1056,256]{1,0:T(8,128)(2,1)S(1)} %collective-permute-done.6.refs_0_, ...), custom_call_target="tpu_custom_call", output_to_operand_aliasing={{0}: (4, {}), {1}: (5, {}), {2}: (6, {})} | custom-call | flops 8589934592 | bytes 10485760 | tf_op jit(solution)/shard_map/remote/pallas_call | solution.py:402
  53.3 0.0 collective-permute-done.9.refs_1_
  53.4 0.0 collective-permute-done.8.refs_0_
  53.4 0.0 slice-done.1
  53.4 0.0 slice-done.2
  53.4 0.0 slice-done.3
  53.4 10.0 %last.1 = (bf16[2880,128]{1,0:T(8,128)(2,1)S(1)}, bf16[2880,128]{1,0:T(8,128)(2,1)S(1)}) custom-call(bf16[2048,256]{1,0:T(8,128)(2,1)S(1)} %copy-done.6, bf16[800,256]{1,0:T(8,128)(2,1)S(1)} %collective-permute-done.8.refs_0_, bf16[784,256]{1,0:T(8,128)(2,1)S(1)} %collective-permute-done.9.refs_1_, f32[16,256]{1,0:T(8,128)S(1)} %get-tuple-element.50.meta.refs_5_.refs_2_, ...), custom_call_target="tpu_custom_call" | custom-call | flops 6442450944 | bytes 10485760 | tf_op jit(solution)/shard_map/last/pallas_call | solution.py:442
  63.4 0.1 collective-permute-start.10
  63.4 2.2 %collective-permute-done.10 = bf16[2880,128]{1,0:T(8,128)(2,1)S(1)} collective-permute-done((bf16[2880,128]{1,0:T(8,128)(2,1)S(1)}, bf16[2880,128]{1,0:T(8,128)(2,1)S(1)}, u32[]{:S(2)}, u32[]{:S(2)}) %collective-permute-start.10) | collective-permute-done | bytes 737312 | tf_op jit(solution)/shard_map/ppermute | solution.py:536
  65.6 1.1 %fusion = bf16[128,2880]{0,1:T(8,128)(2,1)} fusion(bf16[2880,128]{1,0:T(8,128)(2,1)S(1)} %collective-permute-done.10, bf16[2880,128]{1,0:T(8,128)(2,1)S(1)} %get-tuple-element.88), kind=kLoop, calls=%fused_computation.1 | loop fusion | flops 1474560 | bytes 2211840 | tf_op jit(solution)/shard_map/transpose | solution.py:538
  (7 shorter events, 0.1 us)
Async XLA Ops:
  0.6 2.5 %copy-start.1 = (bf16[256,2048]{1,0:T(8,128)(2,1)S(1)}, bf16[256,2048]{1,0:T(8,128)(2,1)}, u32[]{:S(2)}) copy-start(bf16[256,2048]{1,0:T(8,128)(2,1)} %fq.1) | copy-start | bytes 3145732
  3.1 8.3 %collective-permute-start = (bf16[528,256]{1,0:T(8,128)(2,1)S(1)}, bf16[528,256]{1,0:T(8,128)(2,1)S(1)}, u32[]{:S(2)}, u32[]{:S(2)}) collective-permute-start(bf16[528,256]{1,0:T(8,128)(2,1)S(1)} %get-tuple-element.64.block), channel_id=1, source_target_pairs={{0,8},{2,10},{4,12},{6,14},{8,16},{10,18},{12,20},{14,22},{16,24},... | collective-permute-start | bytes 811016 | tf_op jit(solution)/shard_map/ppermute | solution.py:465
  3.1 1.2 %copy-start.2 = (bf16[256,2048]{1,0:T(8,128)(2,1)S(1)}, bf16[256,2048]{1,0:T(8,128)(2,1)}, u32[]{:S(2)}) copy-start(bf16[256,2048]{1,0:T(8,128)(2,1)} %bq.1) | copy-start | bytes 3145732
  7.9 1.4 %copy-start.3 = (f32[2048,256]{1,0:T(8,128)}, f32[2048,256]{1,0:T(8,128)S(1)}, u32[]{:S(2)}) copy-start(f32[2048,256]{1,0:T(8,128)S(1)} %get-tuple-element.71.refs_8_) | copy-start | bytes 6291460
  9.3 1.0 %copy-start.5 = (bf16[2048,256]{1,0:T(8,128)(2,1)}, bf16[2048,256]{1,0:T(8,128)(2,1)S(1)}, u32[]{:S(2)}) copy-start(bf16[2048,256]{1,0:T(8,128)(2,1)S(1)} %get-tuple-element.60.fqt) | copy-start | bytes 3145732
  11.3 7.7 %collective-permute-start.3 = (bf16[528,128]{1,0:T(8,128)(2,1)S(1)}, bf16[528,128]{1,0:T(8,128)(2,1)S(1)}, u32[]{:S(2)}, u32[]{:S(2)}) collective-permute-start(bf16[528,128]{1,0:T(8,128)(2,1)S(1)} %get-tuple-element.58), channel_id=1, source_target_pairs={{0,2},{2,4},{4,6},{6,8},{8,10},{10,12},{12,14},{14,16},{16,18},{18... | collective-permute-start | bytes 405512 | tf_op jit(solution)/shard_map/ppermute | solution.py:465
  12.8 10.6 %collective-permute-start.1 = (bf16[528,256]{1,0:T(8,128)(2,1)S(1)}, bf16[528,256]{1,0:T(8,128)(2,1)S(1)}, u32[]{:S(2)}, u32[]{:S(2)}) collective-permute-start(bf16[528,256]{1,0:T(8,128)(2,1)S(1)} %collective-permute-done.refs_0_), channel_id=1, source_target_pairs={{8,16},{10,18},{12,20},{14,22},{16,24},{18,26},{20,28},{22,30},{9,... | collective-permute-start | bytes 811016 | tf_op jit(solution)/shard_map/ppermute | solution.py:465
  14.1 14.4 %collective-permute-start.2 = (bf16[528,256]{1,0:T(8,128)(2,1)S(1)}, bf16[528,256]{1,0:T(8,128)(2,1)S(1)}, u32[]{:S(2)}, u32[]{:S(2)}) collective-permute-start(bf16[528,256]{1,0:T(8,128)(2,1)S(1)} %collective-permute-done.refs_0_), channel_id=1, source_target_pairs={{8,24},{10,26},{12,28},{14,30},{9,25},{11,27},{13,29},{15,31}} | collective-permute-start | bytes 811016 | tf_op jit(solution)/shard_map/ppermute | solution.py:465
  15.4 13.1 %collective-permute-start.4 = (bf16[528,256]{1,0:T(8,128)(2,1)S(1)}, bf16[528,256]{1,0:T(8,128)(2,1)S(1)}, u32[]{:S(2)}, u32[]{:S(2)}) collective-permute-start(bf16[528,256]{1,0:T(8,128)(2,1)S(1)} %collective-permute-done.refs_0_), channel_id=1, source_target_pairs={{0,2},{2,0},{4,6},{6,4},{8,10},{10,8},{12,14},{14,12},{16,18},{18,... | collective-permute-start | bytes 811016 | tf_op jit(solution)/shard_map/ppermute | solution.py:470
  17.0 11.6 %collective-permute-start.5 = (bf16[528,256]{1,0:T(8,128)(2,1)S(1)}, bf16[528,256]{1,0:T(8,128)(2,1)S(1)}, u32[]{:S(2)}, u32[]{:S(2)}) collective-permute-start(bf16[528,256]{1,0:T(8,128)(2,1)S(1)} %collective-permute-done.refs_0_), channel_id=1, source_target_pairs={{0,4},{2,6},{4,0},{6,2},{8,12},{10,14},{12,8},{14,10},{16,20},{18,... | collective-permute-start | bytes 811016 | tf_op jit(solution)/shard_map/ppermute | solution.py:470
  28.5 3.1 %copy-start = (bf16[528,256]{1,0:T(8,128)(2,1)}, bf16[528,256]{1,0:T(8,128)(2,1)S(1)}, u32[]{:S(2)}) copy-start(bf16[528,256]{1,0:T(8,128)(2,1)S(1)} %collective-permute-done.5.refs_2_) | copy-start | bytes 811012
  28.5 3.1 %copy-start.6 = (bf16[2048,256]{1,0:T(8,128)(2,1)S(1)}, bf16[2048,256]{1,0:T(8,128)(2,1)}, u32[]{:S(2)}) copy-start(bf16[2048,256]{1,0:T(8,128)(2,1)} %copy-done.5) | copy-start | bytes 3145732
  28.6 3.1 %copy-start.4 = (f32[2048,256]{1,0:T(8,128)S(1)}, f32[2048,256]{1,0:T(8,128)}, u32[]{:S(2)}) copy-start(f32[2048,256]{1,0:T(8,128)} %copy-done.3) | copy-start | bytes 6291460
  28.7 13.0 %collective-permute-start.6 = (bf16[1056,256]{1,0:T(8,128)(2,1)S(1)}, bf16[1056,256]{1,0:T(8,128)(2,1)S(1)}, u32[]{:S(2)}, u32[]{:S(2)}) collective-permute-start(bf16[1056,256]{1,0:T(8,128)(2,1)S(1)} %get-tuple-element.93), channel_id=1, source_target_pairs={{0,2},{2,0},{4,6},{6,4},{8,10},{10,8},{12,14},{14,12},{16,18},{18,... | collective-permute-start | bytes 1622024 | tf_op jit(solution)/shard_map/ppermute | solution.py:470
  30.2 12.3 %collective-permute-start.7 = (bf16[1056,256]{1,0:T(8,128)(2,1)S(1)}, bf16[1056,256]{1,0:T(8,128)(2,1)S(1)}, u32[]{:S(2)}, u32[]{:S(2)}) collective-permute-start(bf16[1056,256]{1,0:T(8,128)(2,1)S(1)} %get-tuple-element.92), channel_id=1, source_target_pairs={{0,4},{2,6},{4,0},{6,2},{8,12},{10,14},{12,8},{14,10},{16,20},{18,... | collective-permute-start | bytes 1622024 | tf_op jit(solution)/shard_map/ppermute | solution.py:470
  41.7 2.5 %slice-start = ((bf16[528,256]{1,0:T(8,128)(2,1)}), bf16[272,256]{1,0:T(8,128)(2,1)S(1)}, s32[]{:S(2)}) async-start(bf16[528,256]{1,0:T(8,128)(2,1)} %copy-done), calls=%async_computation | async-start | bytes 278528 | tf_op jit(solution)/shard_map/slice | solution.py:511
  42.6 10.7 %collective-permute-start.9 = (bf16[784,256]{1,0:T(8,128)(2,1)S(1)}, bf16[784,256]{1,0:T(8,128)(2,1)S(1)}, u32[]{:S(2)}, u32[]{:S(2)}) collective-permute-start(bf16[784,256]{1,0:T(8,128)(2,1)S(1)} %pad_maximum_fusion.4), channel_id=1, source_target_pairs={{0,4},{2,6},{4,0},{6,2},{8,12},{10,14},{12,8},{14,10},{16,20},{18,... | collective-permute-start | bytes 1204232 | tf_op jit(solution)/shard_map/ppermute | solution.py:470
  44.2 9.2 %slice-start.1 = ((s8[11796480]{0:T(1024)(128)(4,1)}), s8[4194304]{0:T(1024)(128)(4,1)S(1)}, s32[]{:S(2)}) async-start(s8[11796480]{0:T(1024)(128)(4,1)} %bitcast.7), calls=%async_computation.1 | async-start | bytes 8388608
  44.2 9.1 %slice-start.2 = ((s8[11796480]{0:T(1024)(128)(4,1)}), s8[4194304]{0:T(1024)(128)(4,1)S(1)}, s32[]{:S(2)}) async-start(s8[11796480]{0:T(1024)(128)(4,1)} %bitcast.7), calls=%async_computation.2 | async-start | bytes 8388608
  44.3 9.1 %slice-start.3 = ((s8[11796480]{0:T(1024)(128)(4,1)}), s8[3407872]{0:T(1024)(128)(4,1)S(1)}, s32[]{:S(2)}) async-start(s8[11796480]{0:T(1024)(128)(4,1)} %bitcast.7), calls=%async_computation.3 | async-start | bytes 6815744
  44.3 9.1 %collective-permute-start.8 = (bf16[800,256]{1,0:T(8,128)(2,1)S(1)}, bf16[800,256]{1,0:T(8,128)(2,1)S(1)}, u32[]{:S(2)}, u32[]{:S(2)}) collective-permute-start(bf16[800,256]{1,0:T(8,128)(2,1)S(1)} %pad_maximum_fusion.3), channel_id=1, source_target_pairs={{0,2},{2,0},{4,6},{6,4},{8,10},{10,8},{12,14},{14,12},{16,18},{18,... | collective-permute-start | bytes 1228808 | tf_op jit(solution)/shard_map/ppermute | solution.py:470
  63.4 2.3 %collective-permute-start.10 = (bf16[2880,128]{1,0:T(8,128)(2,1)S(1)}, bf16[2880,128]{1,0:T(8,128)(2,1)S(1)}, u32[]{:S(2)}, u32[]{:S(2)}) collective-permute-start(bf16[2880,128]{1,0:T(8,128)(2,1)S(1)} %get-tuple-element.89), channel_id=1, source_target_pairs={{0,1},{1,0},{2,3},{3,2},{4,5},{5,4},{6,7},{7,6},{8,9},{9,8},{10,11... | collective-permute-start | bytes 2211848 | tf_op jit(solution)/shard_map/ppermute | solution.py:536
